TPU v7x, 32 devices: a whole 2x2x4 slice. The times are simulated.
32 devices in a mesh: pages: 2 (over y), rows: 4 (over x, core), cols: 4 (over z).
Axes of the slice: x: 2, y: 2, z: 4, core: 2. Of those that a mesh axis runs over, the one named last changes fastest.
Arguments:
- features: bfloat16 [128, 64, 768], P(('pages', 'rows'), 'cols'), parts along dimension 0, may hold values from -6 to 6
- dw_kernel: bfloat16 [31, 31, 768], P(None, None, ('rows', 'cols')), may hold values from -0.1875 to 0.1875
- w_up: bfloat16 [768, 1536], P(None, ('rows', 'cols')), may hold values from -0.21875 to 0.21875
- w_down: bfloat16 [768, 1536], P(None, ('rows', 'cols')), may hold values from -0.15625 to 0.15625
Outputs:
- block_out: bfloat16 [128, 64, 768], P(('pages', 'rows'), 'cols'), parts along dimension 0
There are 2 independent parts, one for each index of `pages`. A program takes and returns all parts, laid end to end along the dimension named above; an argument that names none is the same for every part. Nothing has to cross between parts.
All inputs are finite; a program needn't handle non-finite values.
Results may differ from a plain program's by a relative error of at most 0.0053.
Values may be sent and summed in bfloat16 or wider, within the bound.
No kernel may reach another device: no remote copies, remote signals or barrier semaphores. Data moves between devices by JAX's collectives and lax.ppermute only.
A program may use at most 64 MiB of HBM per device.

v0:
```python
import jax
import jax.numpy as jnp
from jax import lax
from jax.experimental import pallas as pl
from jax.experimental.pallas import tpu as pltpu
from jax.sharding import PartitionSpec as P

LANES = 128
STEP = 8
BUILD = 8
CONV = 16


def per_step(count, most):
    return max(n for n in range(1, most + 1) if count % n == 0)


def toeplitz_kernel(v_ref, out_ref, *, half, width):
    count, steps, tiles, _ = v_ref.shape
    block = 16
    lane = lax.broadcasted_iota(jnp.int32, (block, LANES), 1) % width
    row = lax.broadcasted_iota(jnp.int32, (block, LANES), 0)
    bands = [jnp.abs(row + start - lane) <= half for start in range(0, width, block)]
    def build(channel, carry):
        for shift in range(steps):
            for tile in range(tiles):
                taps = v_ref[channel, shift, tile : tile + 1, :]
                taps = jnp.broadcast_to(taps.astype(jnp.float32), (block, LANES))
                turned = pltpu.roll(taps, LANES - half, axis=1, stride=1, stride_axis=0)
                for index, band in enumerate(bands):
                    start = index * block
                    piece = turned if start == 0 else pltpu.roll(turned, start, axis=1)
                    out_ref[
                        channel,
                        shift * width + start : shift * width + start + block,
                        tile * LANES : (tile + 1) * LANES,
                    ] = jnp.where(band, piece, 0.0).astype(jnp.bfloat16)
        return carry

    lax.fori_loop(0, count, build, 0)


def conv_kernel(matrix_ref, img_ref, out_ref, shifted, *, half, segs):
    count, height, width = img_ref.shape
    tiles = matrix_ref.shape[2] // LANES
    rows = height + STEP * (tiles * segs - 1)

    @pl.when(pl.program_id(0) == 0)
    def _():
        shifted[...] = jnp.zeros_like(shifted)

    for channel in range(count):
        x = img_ref[channel].astype(jnp.float32)
        for seg in range(segs):
            shifted[
                channel, half - seg : half - seg + height, seg * width : (seg + 1) * width
            ] = x
        left = jnp.concatenate(
            [
                shifted[channel, s : s + rows, :].astype(jnp.bfloat16)
                for s in range(0, STEP, segs)
            ],
            axis=1,
        )
        product = jnp.dot(left, matrix_ref[channel], preferred_element_type=jnp.float32)
        keep = height + STEP * (segs - 1)
        total = product[:keep, :LANES]
        for tile in range(1, tiles):
            start = tile * segs * STEP
            total = total + product[start : start + keep, tile * LANES : (tile + 1) * LANES]
        mixed = total[:height, :width]
        for seg in range(1, segs):
            part = total[seg * STEP : seg * STEP + height, :]
            mixed = mixed + pltpu.roll(part, LANES - seg * width, axis=1)[:, :width]
        out_ref[channel] = (x + mixed).astype(out_ref.dtype)


def matrices_of(taps, width):
    side, _, count = taps.shape
    half = (side - 1) // 2
    segs = LANES // width
    groups = -(-side // (STEP * segs)) * segs
    v = jnp.transpose(taps[:, ::-1, :], (2, 0, 1))
    v = jnp.pad(v, ((0, 0), (0, STEP * groups - side), (0, width - side)))
    v = v.reshape(count, groups, STEP, width).transpose(0, 2, 1, 3)
    v = v.reshape(count, STEP, groups // segs, LANES)
    several = per_step(count, BUILD)
    shape = (STEP * width, groups * width)
    return pl.pallas_call(
        lambda *refs: toeplitz_kernel(*refs, half=half, width=width),
        grid=(count // several,),
        in_specs=[pl.BlockSpec((several,) + v.shape[1:], lambda i: (i, 0, 0, 0))],
        out_specs=pl.BlockSpec((several,) + shape, lambda i: (i, 0, 0)),
        out_shape=jax.ShapeDtypeStruct((count,) + shape, taps.dtype),
        cost_estimate=pl.CostEstimate(
            flops=count * shape[0] * shape[1] * 4,
            transcendentals=0,
            bytes_accessed=count * shape[0] * shape[1] * 2,
        ),
        name="toeplitz",
    )(v)


def spread_of(matrices, images, half):
    count, height, width = images.shape
    segs = LANES // width
    groups = matrices.shape[2] // width
    several = per_step(count, CONV)
    return pl.pallas_call(
        lambda *refs: conv_kernel(*refs, half=half, segs=segs),
        grid=(count // several,),
        in_specs=[
            pl.BlockSpec((several,) + matrices.shape[1:], lambda i: (i, 0, 0)),
            pl.BlockSpec((several, height, width), lambda i: (i, 0, 0)),
        ],
        out_specs=pl.BlockSpec((several, height, width), lambda i: (i, 0, 0)),
        out_shape=jax.ShapeDtypeStruct(images.shape, images.dtype),
        scratch_shapes=[pltpu.VMEM((several, height + STEP * groups, LANES), jnp.float32)],
        name="depthwise",
    )(matrices, images)


def on_device(features, dw_kernel, w_up, w_down):
    axes = ("rows", "cols")
    down = lax.axis_size("rows")
    across = lax.axis_size("cols")
    devices = down * across
    tile_rows, tile_cols, channels = features.shape
    cells = tile_rows * tile_cols
    own = channels // devices
    weights = jnp.concatenate([w_up.T, w_down.T], axis=0)
    weights = lax.all_gather(weights, axes, axis=0)
    piece = w_up.shape[1]
    turned = features.reshape(cells, channels).T.reshape(devices, own, cells)
    matrices = matrices_of(dw_kernel, across * tile_cols)
    images = lax.all_to_all(turned, axes, 0, 0, tiled=True)
    images = images.reshape(down, across, own, tile_rows, tile_cols)
    images = images.transpose(2, 0, 3, 1, 4).reshape(own, down * tile_rows, across * tile_cols)
    spread = spread_of(matrices, images, (dw_kernel.shape[0] - 1) // 2)
    spread = spread.reshape(own, down, tile_rows, across, tile_cols)
    spread = spread.transpose(1, 3, 0, 2, 4).reshape(devices, own, cells)
    spread = lax.all_to_all(spread, axes, 0, 0, tiled=True)
    values = spread.reshape(channels, cells).T.astype(jnp.float32)
    center = jnp.mean(values, axis=1, keepdims=True)
    spread_sq = jnp.mean((values - center) ** 2, axis=1, keepdims=True)
    normed = ((values - center) * lax.rsqrt(spread_sq + 1e-06)).astype(jnp.bfloat16)
    up = weights[:, :piece].reshape(devices * piece, channels)
    back = weights[:, piece:].reshape(devices * piece, channels)
    hidden = jax.nn.gelu(
        lax.dot_general(
            normed, up, (((1,), (1,)), ((), ())), preferred_element_type=jnp.float32
        ),
        approximate=False,
    ).astype(jnp.bfloat16)
    ffn = jnp.dot(hidden, back, preferred_element_type=jnp.float32)
    result = (values + ffn).astype(jnp.bfloat16)
    return result.reshape(tile_rows, tile_cols, channels)


def solution(mesh):
    return jax.shard_map(
        on_device,
        mesh=mesh,
        in_specs=(
            P(("pages", "rows"), "cols", None),
            P(None, None, ("rows", "cols")),
            P(None, ("rows", "cols")),
            P(None, ("rows", "cols")),
        ),
        out_specs=P(("pages", "rows"), "cols", None),
        check_vma=False,
    )
```

profile of v0, /device:TPU:0, one launch (start us, length us, event | category | flops | bytes accessed | tf_op | source)
XLA Modules:
  0.0 94.8 jit_solution(12062557488680187877)
XLA Ops:
  6.5 1.8 %pad_maximum_fusion = bf16[192,768]{1,0:T(8,128)(2,1)} fusion(bf16[96,768]{1,0:T(8,128)(2,1)} %bitcast.49, bf16[96,768]{1,0:T(8,128)(2,1)} %bitcast.50), kind=kLoop, calls=%fused_computation.56 | loop fusion | flops 589824 | bytes 589824 | tf_op jit(solution)/shard_map/concatenate | solution.py:131
  8.3 0.0 all-gather.3.cloned.1.call-update
  8.3 1.9 %copy.25 = bf16[768,256]{1,0:T(8,128)(2,1)} copy(bf16[768,256]{0,1:T(8,128)(2,1)} %bitcast.48) | data formatting | bytes 786432 | tf_op jit(solution)/shard_map/transpose | solution.py:134
  10.3 7.4 %all-to-all-start = ((bf16[16,48,256]{2,1,0:T(8,128)(2,1)}), bf16[16,48,256]{2,1,0:T(8,128)(2,1)S(1)}, u32[]{:S(2)}, u32[]{:S(2)}) async-start(bf16[16,48,256]{2,1,0:T(8,128)(2,1)} %bitcast.5), calls=%async_computation | async-start | bytes 786432 | tf_op jit(solution)/shard_map/all_to_all | solution.py:136
  17.7 0.2 rev.3
  17.9 0.1 pad.4
  18.0 0.6 copy.24
  18.6 0.9 reshape.48.refs_0_
  19.5 11.6 %toeplitz.1.refs_0_ = bf16[48,512,256]{2,1,0:T(8,128)(2,1)} custom-call(bf16[48,8,2,128]{3,2,1,0:T(2,128)(2,1)} %reshape.48.refs_0_), custom_call_target="tpu_custom_call" | custom-call | flops 25165824 | bytes 12582912 | tf_op jit(solution)/shard_map/toeplitz/pallas_call | solution.py:89
  31.1 5.5 %all-to-all-done = bf16[16,48,256]{2,1,0:T(8,128)(2,1)S(1)} async-done(((bf16[16,48,256]{2,1,0:T(8,128)(2,1)}), bf16[16,48,256]{2,1,0:T(8,128)(2,1)S(1)}, u32[]{:S(2)}, u32[]{:S(2)}) %all-to-all-start) | async-done | bytes 393248 | tf_op jit(solution)/shard_map/all_to_all | solution.py:136
  36.6 0.5 copy.26
  37.1 0.3 copy.27
  37.4 2.0 %copy.28.refs_1_ = bf16[48,64,64]{2,1,0:T(8,128)(2,1)} copy(bf16[48,64,64]{0,2,1:T(8,128)(2,1)S(1)} %bitcast.38) | data formatting | bytes 786432 | tf_op jit(solution)/shard_map/reshape | solution.py:138
  39.4 7.5 %depthwise.1 = bf16[48,64,64]{2,1,0:T(8,128)(2,1)} custom-call(bf16[48,512,256]{2,1,0:T(8,128)(2,1)} %toeplitz.1.refs_0_, bf16[48,64,64]{2,1,0:T(8,128)(2,1)} %copy.28.refs_1_), custom_call_target="tpu_custom_call" | custom-call | tf_op jit(solution)/shard_map/depthwise/pallas_call | solution.py:109
  46.9 1.9 %copy.29 = bf16[48,64,64]{0,2,1:T(8,128)(2,1)S(1)} copy(bf16[48,64,64]{2,1,0:T(8,128)(2,1)} %depthwise.1) | data formatting | bytes 786432 | tf_op jit(solution)/shard_map/depthwise/pallas_call | solution.py:109
  48.8 0.3 copy.30
  49.1 0.3 copy.31
  49.4 25.6 %all_to_all.10 = bf16[16,48,256]{2,1,0:T(8,128)(2,1)S(1)} all-to-all(bf16[16,48,256]{2,1,0:T(8,128)(2,1)S(1)} %copy.31), channel_id=1, replica_groups=mesh['pages'=2,'rows'=4,'cols'=4] {'rows','cols'}, dimensions={0} | all-to-all | bytes 786432 | tf_op jit(solution)/shard_map/all_to_all | solution.py:142
  75.0 0.2 copy.32
  75.2 0.1 convert_reduce_fusion
  75.3 0.2 multiply_reduce_fusion
  75.5 1.3 %all-gather.3.cloned.1.call-done = bf16[3072,768]{1,0:T(8,128)(2,1)} async-done(((bf16[192,768]{1,0:T(8,128)(2,1)}), bf16[3072,768]{1,0:T(8,128)(2,1)}) %all-gather.3.cloned.1.call-update) | async-done | bytes 4718608 | tf_op jit(solution)/shard_map/all_gather | solution.py:132
  76.8 4.1 %fusion.76 = (bf16[16,96,768]{2,1,0:T(8,128)(2,1)S(1)}, bf16[16,96,768]{2,1,0:T(8,128)(2,1)}) fusion(bf16[16,192,768]{2,1,0:T(8,128)(2,1)} %bitcast.37), kind=kLoop, calls=%fused_computation.90 | loop fusion | bytes 9437184 | tf_op jit(solution)/shard_map/slice | solution.py:147
  80.9 7.0 %fusion.10 = bf16[256,768]{1,0:T(8,128)(2,1)} fusion(bf16[1536,768]{1,0:T(8,128)(2,1)} %bitcast.44, f32[768,256]{0,1:T(8,128)S(1)} %copy.32, bf16[1536,768]{1,0:T(8,128)(2,1)S(1)} %bitcast.43, f32[256]{0:T(256)S(1)} %add_rsqrt_fusion, f32[256]{0:T(256)S(1)} %broadcast_multiply_fusion), kind=kOutput, calls=%fused_computation.20 | convolution fusion | flops 1234501632 | bytes 5900288 | tf_op jit(solution)/shard_map/dot_general | solution.py:155
  (5 shorter events, 0.0 us)
Async XLA Ops:
  6.5 11.1 %copy-start = (bf16[31,31,48]{2,1,0:T(8,128)(2,1)S(1)}, bf16[31,31,48]{2,1,0:T(8,128)(2,1)}, u32[]{:S(2)}) copy-start(bf16[31,31,48]{2,1,0:T(8,128)(2,1)} %param.5) | copy-start | bytes 276772
  6.5 70.3 %all-gather.3.cloned.1.call-start = ((), (), s32[]{:S(2)}) async-start(), calls=%async_computation.2 | async-start | bytes 5013504 | tf_op jit(solution)/shard_map/all_gather | solution.py:132
  10.3 26.3 %all-to-all-start = ((bf16[16,48,256]{2,1,0:T(8,128)(2,1)}), bf16[16,48,256]{2,1,0:T(8,128)(2,1)S(1)}, u32[]{:S(2)}, u32[]{:S(2)}) async-start(bf16[16,48,256]{2,1,0:T(8,128)(2,1)} %bitcast.5), calls=%async_computation | async-start | bytes 786432 | tf_op jit(solution)/shard_map/all_to_all | solution.py:136
Sparse Core Ops, SparseCore 0:
  9.6 67.1 all-gather.2
where the time goes:
time: 95.2 us; the launch traced here: 94.8 us
  blocking collectives  25.6 us (27%)
  Pallas kernels  19.1 us (20%)
  between operations  13.5 us (14%)
  local copies, waits for them, and re-layouts  13.3 us (14%)
  starting transfers between devices  7.39 us (8%)
  matrix products  7.03 us (7%)
  waiting for transfers between devices  6.81 us (7%)
  other arithmetic  2.14 us (2%)
    all_to_all x1, blocking collectives, on_device(): spread = lax.all_to_all(spread, axes, 0, 0, tiled=True)  25.6 us
    pallas_call x1, Pallas kernels, matrices_of(): pl.pallas_call(lambda *refs: toeplitz_kernel(*refs, half=half, width=widt...  11.6 us
    pallas_call x1, Pallas kernels, spread_of(): pl.pallas_call(lambda *refs: conv_kernel(*refs, half=half, segs=segs), gr...  7.45 us
    all_to_all x1, starting transfers between devices, on_device(): images = lax.all_to_all(turned, axes, 0, 0, tiled=True)  7.39 us
    dot_general x1, matrix products, on_device(): ffn = jnp.dot(hidden, back, preferred_element_type=jnp.float32)  7.03 us
    all_to_all x1, waiting for transfers between devices, on_device(): images = lax.all_to_all(turned, axes, 0, 0, tiled=True)  5.5 us
    slice x1, local copies, waits for them, and re-layouts, on_device(): up = weights[:, :piece].reshape(devices * piece, channels)  4.1 us
    reshape x1, local copies, waits for them, and re-layouts, on_device(): images.transpose(2, 0, 3, 1, 4)  2.01 us
  transfers between devices with their start and end apart: 2, of which 2 were waited for; matrix products, arithmetic and copies ran while one was open for 10% of the time, Pallas kernels for 20%

commit v1 on v0

--- a/solution.py
+++ b/solution.py
@@ -21,6 +21,7 @@
     lane = lax.broadcasted_iota(jnp.int32, (block, LANES), 1) % width
     row = lax.broadcasted_iota(jnp.int32, (block, LANES), 0)
     bands = [jnp.abs(row + start - lane) <= half for start in range(0, width, block)]
+
     def build(channel, carry):
         for shift in range(steps):
             for tile in range(tiles):
@@ -120,6 +121,78 @@
     )(matrices, images)
 
 
+def add_hidden(total, normed, piece_refs):
+    for ref in piece_refs:
+        count, _, units, channels = ref.shape
+        up = ref[:, 0].reshape(count * units, channels)
+        down = ref[:, 1].reshape(count * units, channels)
+        hidden = lax.dot_general(
+            normed, up, (((1,), (1,)), ((), ())), preferred_element_type=jnp.float32
+        )
+        hidden = (0.5 * hidden * (1.0 + lax.erf(hidden * 0.5**0.5))).astype(jnp.bfloat16)
+        total = total + jnp.dot(hidden, down, preferred_element_type=jnp.float32)
+    return total
+
+
+def first_kernel(*refs):
+    spread_ref, *piece_refs, normed_ref, total_ref = refs
+    values = spread_ref[...].astype(jnp.float32).T
+    center = jnp.mean(values, axis=1, keepdims=True)
+    spread_sq = jnp.mean((values - center) ** 2, axis=1, keepdims=True)
+    normed = ((values - center) * lax.rsqrt(spread_sq + 1e-06)).astype(jnp.bfloat16)
+    normed_ref[...] = normed
+    total_ref[...] = add_hidden(values, normed, piece_refs)
+
+
+def second_kernel(*refs):
+    normed_ref, total_ref, *piece_refs, out_ref = refs
+    total = add_hidden(total_ref[...], normed_ref[...], piece_refs)
+    out_ref[...] = total.astype(out_ref.dtype)
+
+
+def aligned(pieces):
+    channels = pieces[0].shape[3]
+    if pieces[0].shape[2] % 16 != 0:
+        joined = jnp.concatenate(pieces, axis=0)
+        pieces = [joined.transpose(1, 0, 2, 3).reshape(1, 2, -1, channels)]
+    return pieces
+
+
+def block_of(spread, near, far):
+    channels, cells = spread.shape
+    near, far = aligned(near), aligned(far)
+    whole = pl.BlockSpec(memory_space=pltpu.VMEM)
+    normed, total = pl.pallas_call(
+        first_kernel,
+        in_specs=[whole] * (1 + len(near)),
+        out_specs=[whole] * 2,
+        out_shape=[
+            jax.ShapeDtypeStruct((cells, channels), spread.dtype),
+            jax.ShapeDtypeStruct((cells, channels), jnp.float32),
+        ],
+        name="feed_forward_near",
+    )(spread, *near)
+    return pl.pallas_call(
+        second_kernel,
+        in_specs=[whole] * (2 + len(far)),
+        out_specs=whole,
+        out_shape=jax.ShapeDtypeStruct((cells, channels), spread.dtype),
+        name="feed_forward_far",
+    )(normed, total, *far)
+
+
+def turn(array, axis, shift, within=1):
+    size = lax.axis_size(axis)
+    return lax.ppermute(
+        array, axis, [(i, (i + shift * within) % size) for i in range(size)]
+    )
+
+
+def partner(array, axis):
+    size = lax.axis_size(axis)
+    return lax.ppermute(array, axis, [(i, i ^ 1) for i in range(size)])
+
+
 def on_device(features, dw_kernel, w_up, w_down):
     axes = ("rows", "cols")
     down = lax.axis_size("rows")
@@ -128,32 +201,31 @@
     tile_rows, tile_cols, channels = features.shape
     cells = tile_rows * tile_cols
     own = channels // devices
-    weights = jnp.concatenate([w_up.T, w_down.T], axis=0)
-    weights = lax.all_gather(weights, axes, axis=0)
-    piece = w_up.shape[1]
+    pages = lax.axis_size("pages")
+    units = w_up.shape[1] // pages
+    piece = jnp.stack([w_up.T, w_down.T])[None]
+    piece = lax.dynamic_slice_in_dim(piece, lax.axis_index("pages") * units, units, axis=2)
+    line = [piece] + [turn(piece, "cols", shift) for shift in range(1, across)]
     turned = features.reshape(cells, channels).T.reshape(devices, own, cells)
+    images = lax.all_to_all(turned, axes, 0, 0, tiled=True)
     matrices = matrices_of(dw_kernel, across * tile_cols)
-    images = lax.all_to_all(turned, axes, 0, 0, tiled=True)
+    images, matrices, line = lax.optimization_barrier((images, matrices, line))
+    line = jnp.concatenate(line, axis=0)
+    others = [turn(line, "rows", shift, 2) for shift in range(1, down // 2)]
+    near = [line] + [turn(line, "pages", shift) for shift in range(1, pages)]
     images = images.reshape(down, across, own, tile_rows, tile_cols)
     images = images.transpose(2, 0, 3, 1, 4).reshape(own, down * tile_rows, across * tile_cols)
     spread = spread_of(matrices, images, (dw_kernel.shape[0] - 1) // 2)
     spread = spread.reshape(own, down, tile_rows, across, tile_cols)
     spread = spread.transpose(1, 3, 0, 2, 4).reshape(devices, own, cells)
+    spread, others, near = lax.optimization_barrier((spread, others, near))
+    near = near + others
+    far = [partner(each, "rows") for each in near]
+    last = [turn(other, "pages", shift) for other in others for shift in range(1, pages)]
     spread = lax.all_to_all(spread, axes, 0, 0, tiled=True)
-    values = spread.reshape(channels, cells).T.astype(jnp.float32)
-    center = jnp.mean(values, axis=1, keepdims=True)
-    spread_sq = jnp.mean((values - center) ** 2, axis=1, keepdims=True)
-    normed = ((values - center) * lax.rsqrt(spread_sq + 1e-06)).astype(jnp.bfloat16)
-    up = weights[:, :piece].reshape(devices * piece, channels)
-    back = weights[:, piece:].reshape(devices * piece, channels)
-    hidden = jax.nn.gelu(
-        lax.dot_general(
-            normed, up, (((1,), (1,)), ((), ())), preferred_element_type=jnp.float32
-        ),
-        approximate=False,
-    ).astype(jnp.bfloat16)
-    ffn = jnp.dot(hidden, back, preferred_element_type=jnp.float32)
-    result = (values + ffn).astype(jnp.bfloat16)
+    spread, last = lax.optimization_barrier((spread, last))
+    far += [partner(each, "rows") for each in last]
+    result = block_of(spread.reshape(channels, cells), near + last, far)
     return result.reshape(tile_rows, tile_cols, channels)
 
 

time: 95.2 us -> 81.8 us (0.86)
  blocking collectives: 25.6 us -> 0 us
  starting transfers between devices: 7.39 us -> 25 us
  between operations: 13.5 us -> 0.17 us
  waiting for transfers between devices: 6.81 us -> 15.3 us
  Pallas kernels: 19.1 us -> 27.3 us
  matrix products: 7.03 us -> 0 us
  other arithmetic: 2.14 us -> 0.94 us
    all_to_all x1 -> x0, blocking collectives: 25.6 us -> none  [on_device(): spread = lax.all_to_all(spread, axes, 0, 0, tiled=True)]
    ppermute x0 -> x10, waiting for transfers between devices: none -> 15.3 us  [the longest x6 15.3 us: turn(): lax.ppermute(array, axis, [(i, (i + shift * within) % size) for i in rang...]
    ppermute x0 -> x10, starting transfers between devices: none -> 11.1 us  [the longest x6 10.4 us: turn(): lax.ppermute(array, axis, [(i, (i + shift * within) % size) for i in rang...]
    pallas_call x0 -> x2, Pallas kernels: none -> 8.36 us  [the longest x1 4.3 us: block_of(): pl.pallas_call(first_kernel, in_specs=[whole] * (1 + len(near)), out_spec...]
    dot_general x1 -> x0, matrix products: 7.03 us -> none  [on_device(): ffn = jnp.dot(hidden, back, preferred_element_type=jnp.float32)]
    all_to_all x0 -> x1, starting transfers between devices: none -> 6.57 us  [on_device(): spread = lax.all_to_all(spread, axes, 0, 0, tiled=True)]
    all_to_all x1, waiting for transfers between devices: 5.5 us -> 0.01 us  [on_device(): images = lax.all_to_all(turned, axes, 0, 0, tiled=True)]
    slice x1 -> x0, local copies, waits for them, and re-layouts: 4.1 us -> none  [on_device(): up = weights[:, :piece].reshape(devices * piece, channels)]
  transfers between devices with their start and end apart: 2 -> 12, of which waited for: 2 -> 3; matrix products, arithmetic and copies ran while one was open for 10% -> 11% of each run, Pallas kernels for 20% -> 29%
where the time goes in v1:
time: 81.8 us; the launch traced here: 81.2 us
  Pallas kernels  27.3 us (33%)
  starting transfers between devices  25 us (31%)
  waiting for transfers between devices  15.3 us (19%)
  local copies, waits for them, and re-layouts  12.5 us (15%)
  other arithmetic  0.94 us (1%)
    ppermute x6, waiting for transfers between devices, turn(): lax.ppermute(array, axis, [(i, (i + shift * within) % size) for i in rang...  15.3 us
    pallas_call x1, Pallas kernels, matrices_of(): pl.pallas_call(lambda *refs: toeplitz_kernel(*refs, half=half, width=widt...  11.7 us
    ppermute x6, starting transfers between devices, turn(): lax.ppermute(array, axis, [(i, (i + shift * within) % size) for i in rang...  10.4 us
    all_to_all x1, starting transfers between devices, on_device(): images = lax.all_to_all(turned, axes, 0, 0, tiled=True)  7.39 us
    pallas_call x1, Pallas kernels, spread_of(): pl.pallas_call(lambda *refs: conv_kernel(*refs, half=half, segs=segs), gr...  7.27 us
    all_to_all x1, starting transfers between devices, on_device(): spread = lax.all_to_all(spread, axes, 0, 0, tiled=True)  6.57 us
    pallas_call x1, Pallas kernels, block_of(): pl.pallas_call(first_kernel, in_specs=[whole] * (1 + len(near)), out_spec...  4.3 us
    pallas_call x1, Pallas kernels, block_of(): pl.pallas_call(second_kernel, in_specs=[whole] * (2 + len(far)), out_spec...  4.06 us
  transfers between devices with their start and end apart: 12, of which 3 were waited for; matrix products, arithmetic and copies ran while one was open for 11% of the time, Pallas kernels for 29%

profile of v1, /device:TPU:0, one launch (start us, length us, event | category | flops | bytes accessed | tf_op | source)
XLA Modules:
  0.0 81.2 jit_solution(6650135412554861749)
XLA Ops:
  0.0 1.9 %copy.23 = bf16[768,256]{1,0:T(8,128)(2,1)} copy(bf16[768,256]{0,1:T(8,128)(2,1)} %bitcast.33) | data formatting | bytes 786432 | tf_op jit(solution)/shard_map/transpose | solution.py:209
  1.9 7.4 %all-to-all-start = ((bf16[16,48,256]{2,1,0:T(8,128)(2,1)}), bf16[16,48,256]{2,1,0:T(8,128)(2,1)S(1)}, u32[]{:S(2)}, u32[]{:S(2)}) async-start(bf16[16,48,256]{2,1,0:T(8,128)(2,1)} %bitcast.2), calls=%async_computation | async-start | bytes 786432 | tf_op jit(solution)/shard_map/all_to_all | solution.py:210
  9.3 0.9 %fusion.1 = bf16[1,2,48,768]{3,2,1,0:T(8,128)(2,1)S(1)} fusion(s32[]{:T(128)S(6)} %select_n.3, bf16[1,96,768]{2,1,0:T(8,128)(2,1)} %bitcast.34, bf16[1,96,768]{2,1,0:T(8,128)(2,1)} %bitcast.35), kind=kLoop, calls=%fused_computation.3 | loop fusion | flops 294912 | bytes 442372 | tf_op jit(solution)/shard_map/dynamic_slice | solution.py:207
  10.3 2.0 %collective-permute-start = (bf16[1,2,48,768]{3,2,1,0:T(8,128)(2,1)S(1)}, bf16[1,2,48,768]{3,2,1,0:T(8,128)(2,1)S(1)}, u32[]{:S(2)}, u32[]{:S(2)}) collective-permute-start(bf16[1,2,48,768]{3,2,1,0:T(8,128)(2,1)S(1)} %fusion.1), channel_id=1, source_target_pairs={{0,1},{1,2},{2,3},{3,0},{4,5},{5,6},{6,7},{7,4},{8,9},{9,10},{10,1... | collective-permute-start | bytes 442376 | tf_op jit(solution)/shard_map/ppermute | solution.py:186
  12.2 2.4 %collective-permute-start.1 = (bf16[1,2,48,768]{3,2,1,0:T(8,128)(2,1)S(1)}, bf16[1,2,48,768]{3,2,1,0:T(8,128)(2,1)S(1)}, u32[]{:S(2)}, u32[]{:S(2)}) collective-permute-start(bf16[1,2,48,768]{3,2,1,0:T(8,128)(2,1)S(1)} %fusion.1), channel_id=1, source_target_pairs={{0,2},{1,3},{2,0},{3,1},{4,6},{5,7},{6,4},{7,5},{8,10},{9,11},{10,... | collective-permute-start | bytes 442376 | tf_op jit(solution)/shard_map/ppermute | solution.py:186
  14.6 1.5 %collective-permute-start.2 = (bf16[1,2,48,768]{3,2,1,0:T(8,128)(2,1)S(1)}, bf16[1,2,48,768]{3,2,1,0:T(8,128)(2,1)S(1)}, u32[]{:S(2)}, u32[]{:S(2)}) collective-permute-start(bf16[1,2,48,768]{3,2,1,0:T(8,128)(2,1)S(1)} %fusion.1), channel_id=1, source_target_pairs={{0,3},{1,0},{2,1},{3,2},{4,7},{5,4},{6,5},{7,6},{8,11},{9,8},{10,9... | collective-permute-start | bytes 442376 | tf_op jit(solution)/shard_map/ppermute | solution.py:186
  16.0 1.1 %rev.3 = bf16[31,31,48]{2,1,0:T(8,128)(2,1)S(1)} reverse(bf16[31,31,48]{2,1,0:T(8,128)(2,1)} %param.5), dimensions={1} | reverse | bytes 184512 | tf_op jit(solution)/shard_map/rev | solution.py:84
  17.3 0.6 copy.24
  17.9 0.9 %reshape.34.refs_0_ = bf16[48,8,2,128]{3,2,1,0:T(2,128)(2,1)} reshape(bf16[48,8,4,64]{3,2,1,0:T(4,128)(2,1)S(1)} %bitcast.30) | data formatting | bytes 393216 | tf_op jit(solution)/shard_map/reshape | solution.py:87
  18.8 11.7 %toeplitz.1.refs_0_ = bf16[48,512,256]{2,1,0:T(8,128)(2,1)} custom-call(bf16[48,8,2,128]{3,2,1,0:T(2,128)(2,1)} %reshape.34.refs_0_), custom_call_target="tpu_custom_call" | custom-call | flops 25165824 | bytes 12582912 | tf_op jit(solution)/shard_map/toeplitz/pallas_call | solution.py:90
  30.5 1.3 %collective-permute-done.1 = bf16[1,2,48,768]{3,2,1,0:T(8,128)(2,1)S(1)} collective-permute-done((bf16[1,2,48,768]{3,2,1,0:T(8,128)(2,1)S(1)}, bf16[1,2,48,768]{3,2,1,0:T(8,128)(2,1)S(1)}, u32[]{:S(2)}, u32[]{:S(2)}) %collective-permute-start.1) | collective-permute-done | bytes 147488 | tf_op jit(solution)/shard_map/ppermute | solution.py:186
  31.9 1.5 %collective-permute-start.3 = (bf16[4,2,48,768]{3,2,1,0:T(8,128)(2,1)S(1)}, bf16[4,2,48,768]{3,2,1,0:T(8,128)(2,1)}, u32[]{:S(2)}, u32[]{:S(2)}) collective-permute-start(bf16[4,2,48,768]{3,2,1,0:T(8,128)(2,1)S(1)} %constant_dynamic-update-slice_fusion.refs_1_), channel_id=1, source_target_pairs={{0,8},{4,12},{8,0},{12,4},{1,9},{5,13},{9,1},{13,5},{2,10},{6,14},... | collective-permute-start | bytes 1769480 | tf_op jit(solution)/shard_map/ppermute | solution.py:186
  33.4 1.5 %collective-permute-start.4 = (bf16[4,2,48,768]{3,2,1,0:T(8,128)(2,1)S(1)}, bf16[4,2,48,768]{3,2,1,0:T(8,128)(2,1)}, u32[]{:S(2)}, u32[]{:S(2)}) collective-permute-start(bf16[4,2,48,768]{3,2,1,0:T(8,128)(2,1)S(1)} %constant_dynamic-update-slice_fusion.refs_1_), channel_id=1, source_target_pairs={{0,16},{16,0},{1,17},{17,1},{2,18},{18,2},{3,19},{19,3},{4,20},{20... | collective-permute-start | bytes 1769480 | tf_op jit(solution)/shard_map/ppermute | solution.py:186
  35.7 2.0 %copy.27.refs_1_ = bf16[48,64,64]{2,1,0:T(8,128)(2,1)} copy(bf16[48,64,64]{0,2,1:T(8,128)(2,1)S(1)} %bitcast.25) | data formatting | bytes 786432 | tf_op jit(solution)/shard_map/reshape | solution.py:217
  37.7 7.3 %depthwise.1 = bf16[48,64,64]{2,1,0:T(8,128)(2,1)} custom-call(bf16[48,512,256]{2,1,0:T(8,128)(2,1)} %toeplitz.1.refs_0_, bf16[48,64,64]{2,1,0:T(8,128)(2,1)} %copy.27.refs_1_), custom_call_target="tpu_custom_call" | custom-call | tf_op jit(solution)/shard_map/depthwise/pallas_call | solution.py:110
  45.0 1.9 %copy.28 = bf16[48,64,64]{0,2,1:T(8,128)(2,1)S(1)} copy(bf16[48,64,64]{2,1,0:T(8,128)(2,1)} %depthwise.1) | data formatting | bytes 786432 | tf_op jit(solution)/shard_map/depthwise/pallas_call | solution.py:110
  47.4 1.1 %copy.30 = bf16[16,48,256]{2,1,0:T(8,128)(2,1)} copy(bf16[16,48,256]{1,2,0:T(8,128)(2,1)S(1)} %bitcast.27) | data formatting | bytes 786432 | tf_op jit(solution)/shard_map/optimization_barrier | solution.py:221
  48.5 6.6 %all-to-all-start.1 = ((bf16[16,48,256]{2,1,0:T(8,128)(2,1)}), bf16[16,48,256]{2,1,0:T(8,128)(2,1)S(1)}, u32[]{:S(2)}, u32[]{:S(2)}) async-start(bf16[16,48,256]{2,1,0:T(8,128)(2,1)} %copy.30), calls=%async_computation.1 | async-start | bytes 786432 | tf_op jit(solution)/shard_map/all_to_all | solution.py:225
  55.1 1.6 %collective-permute-start.5 = (bf16[4,2,48,768]{3,2,1,0:T(8,128)(2,1)}, bf16[4,2,48,768]{3,2,1,0:T(8,128)(2,1)S(1)}, u32[]{:S(2)}, u32[]{:S(2)}) collective-permute-start(bf16[4,2,48,768]{3,2,1,0:T(8,128)(2,1)} %collective-permute-done.3.refs_3_), channel_id=1, source_target_pairs={{0,16},{16,0},{1,17},{17,1},{2,18},{18,2},{3,19},{19,3},{4,20},{20... | collective-permute-start | bytes 1769480 | tf_op jit(solution)/shard_map/ppermute | solution.py:186
  57.2 13.7 %collective-permute-done.5.refs_4_ = bf16[4,2,48,768]{3,2,1,0:T(8,128)(2,1)S(1)} collective-permute-done((bf16[4,2,48,768]{3,2,1,0:T(8,128)(2,1)}, bf16[4,2,48,768]{3,2,1,0:T(8,128)(2,1)S(1)}, u32[]{:S(2)}, u32[]{:S(2)}) %collective-permute-start.5) | collective-permute-done | bytes 589856 | tf_op jit(solution)/shard_map/ppermute | solution.py:186
  71.0 0.7 copy-done.3
  71.9 4.3 %feed_forward_near.1 = (bf16[256,768]{1,0:T(8,128)(2,1)}, f32[256,768]{1,0:T(8,128)}) custom-call(bf16[768,256]{1,0:T(8,128)(2,1)} %bitcast.31, bf16[4,2,48,768]{3,2,1,0:T(8,128)(2,1)} %copy-done.1, bf16[4,2,48,768]{3,2,1,0:T(8,128)(2,1)} %collective-permute-done.4.refs_2_, bf16[4,2,48,768]{3,2,1,0:T(8,128)(2,1)} %collective-permute-done.3.refs_3_, ...), custom_call_target="tpu_custom_call" | custom-call | tf_op jit(solution)/shard_map/feed_forward_near/pallas_call | solution.py:165
  76.2 0.8 copy-done.4
  77.2 4.1 %feed_forward_far.1 = bf16[256,768]{1,0:T(8,128)(2,1)} custom-call(bf16[256,768]{1,0:T(8,128)(2,1)} %get-tuple-element.31.refs_0_, f32[256,768]{1,0:T(8,128)} %get-tuple-element.32.refs_1_, bf16[4,2,48,768]{3,2,1,0:T(8,128)(2,1)} %copy-done.4, bf16[4,2,48,768]{3,2,1,0:T(8,128)(2,1)} %collective-permute-done.7.refs_3_, bf16[4,2,48,768]{3,2,1,0:T(8,128)(2,1)} %copy-done.2, ...), custom_call_target="tpu_custom_call" | custom-call | tf_op jit(solution)/shard_map/feed_forward_far/pallas_call | solution.py:175
  (30 shorter events, 2.4 us)
Async XLA Ops:
  1.9 29.9 %all-to-all-start = ((bf16[16,48,256]{2,1,0:T(8,128)(2,1)}), bf16[16,48,256]{2,1,0:T(8,128)(2,1)S(1)}, u32[]{:S(2)}, u32[]{:S(2)}) async-start(bf16[16,48,256]{2,1,0:T(8,128)(2,1)} %bitcast.2), calls=%async_computation | async-start | bytes 786432 | tf_op jit(solution)/shard_map/all_to_all | solution.py:210
  10.3 20.2 %collective-permute-start = (bf16[1,2,48,768]{3,2,1,0:T(8,128)(2,1)S(1)}, bf16[1,2,48,768]{3,2,1,0:T(8,128)(2,1)S(1)}, u32[]{:S(2)}, u32[]{:S(2)}) collective-permute-start(bf16[1,2,48,768]{3,2,1,0:T(8,128)(2,1)S(1)} %fusion.1), channel_id=1, source_target_pairs={{0,1},{1,2},{2,3},{3,0},{4,5},{5,6},{6,7},{7,4},{8,9},{9,10},{10,1... | collective-permute-start | bytes 442376 | tf_op jit(solution)/shard_map/ppermute | solution.py:186
  12.2 19.6 %collective-permute-start.1 = (bf16[1,2,48,768]{3,2,1,0:T(8,128)(2,1)S(1)}, bf16[1,2,48,768]{3,2,1,0:T(8,128)(2,1)S(1)}, u32[]{:S(2)}, u32[]{:S(2)}) collective-permute-start(bf16[1,2,48,768]{3,2,1,0:T(8,128)(2,1)S(1)} %fusion.1), channel_id=1, source_target_pairs={{0,2},{1,3},{2,0},{3,1},{4,6},{5,7},{6,4},{7,5},{8,10},{9,11},{10,... | collective-permute-start | bytes 442376 | tf_op jit(solution)/shard_map/ppermute | solution.py:186
  14.6 17.2 %collective-permute-start.2 = (bf16[1,2,48,768]{3,2,1,0:T(8,128)(2,1)S(1)}, bf16[1,2,48,768]{3,2,1,0:T(8,128)(2,1)S(1)}, u32[]{:S(2)}, u32[]{:S(2)}) collective-permute-start(bf16[1,2,48,768]{3,2,1,0:T(8,128)(2,1)S(1)} %fusion.1), channel_id=1, source_target_pairs={{0,3},{1,0},{2,1},{3,2},{4,7},{5,4},{6,5},{7,6},{8,11},{9,8},{10,9... | collective-permute-start | bytes 442376 | tf_op jit(solution)/shard_map/ppermute | solution.py:186
  31.9 24.9 %copy-start.1 = (bf16[4,2,48,768]{3,2,1,0:T(8,128)(2,1)}, bf16[4,2,48,768]{3,2,1,0:T(8,128)(2,1)S(1)}, u32[]{:S(2)}) copy-start(bf16[4,2,48,768]{3,2,1,0:T(8,128)(2,1)S(1)} %constant_dynamic-update-slice_fusion.refs_1_) | copy-start | bytes 1769476
  31.9 15.3 %collective-permute-start.3 = (bf16[4,2,48,768]{3,2,1,0:T(8,128)(2,1)S(1)}, bf16[4,2,48,768]{3,2,1,0:T(8,128)(2,1)}, u32[]{:S(2)}, u32[]{:S(2)}) collective-permute-start(bf16[4,2,48,768]{3,2,1,0:T(8,128)(2,1)S(1)} %constant_dynamic-update-slice_fusion.refs_1_), channel_id=1, source_target_pairs={{0,8},{4,12},{8,0},{12,4},{1,9},{5,13},{9,1},{13,5},{2,10},{6,14},... | collective-permute-start | bytes 1769480 | tf_op jit(solution)/shard_map/ppermute | solution.py:186
  33.4 14.0 %collective-permute-start.4 = (bf16[4,2,48,768]{3,2,1,0:T(8,128)(2,1)S(1)}, bf16[4,2,48,768]{3,2,1,0:T(8,128)(2,1)}, u32[]{:S(2)}, u32[]{:S(2)}) collective-permute-start(bf16[4,2,48,768]{3,2,1,0:T(8,128)(2,1)S(1)} %constant_dynamic-update-slice_fusion.refs_1_), channel_id=1, source_target_pairs={{0,16},{16,0},{1,17},{17,1},{2,18},{18,2},{3,19},{19,3},{4,20},{20... | collective-permute-start | bytes 1769480 | tf_op jit(solution)/shard_map/ppermute | solution.py:186
  48.5 22.4 %all-to-all-start.1 = ((bf16[16,48,256]{2,1,0:T(8,128)(2,1)}), bf16[16,48,256]{2,1,0:T(8,128)(2,1)S(1)}, u32[]{:S(2)}, u32[]{:S(2)}) async-start(bf16[16,48,256]{2,1,0:T(8,128)(2,1)} %copy.30), calls=%async_computation.1 | async-start | bytes 786432 | tf_op jit(solution)/shard_map/all_to_all | solution.py:225
  55.1 15.9 %collective-permute-start.5 = (bf16[4,2,48,768]{3,2,1,0:T(8,128)(2,1)}, bf16[4,2,48,768]{3,2,1,0:T(8,128)(2,1)S(1)}, u32[]{:S(2)}, u32[]{:S(2)}) collective-permute-start(bf16[4,2,48,768]{3,2,1,0:T(8,128)(2,1)} %collective-permute-done.3.refs_3_), channel_id=1, source_target_pairs={{0,16},{16,0},{1,17},{17,1},{2,18},{18,2},{3,19},{19,3},{4,20},{20... | collective-permute-start | bytes 1769480 | tf_op jit(solution)/shard_map/ppermute | solution.py:186
  56.7 19.5 %collective-permute-start.8 = (bf16[4,2,48,768]{3,2,1,0:T(8,128)(2,1)}, bf16[4,2,48,768]{3,2,1,0:T(8,128)(2,1)S(1)}, u32[]{:S(2)}, u32[]{:S(2)}) collective-permute-start(bf16[4,2,48,768]{3,2,1,0:T(8,128)(2,1)} %collective-permute-done.3.refs_3_), channel_id=1, source_target_pairs={{0,4},{4,0},{8,12},{12,8},{1,5},{5,1},{9,13},{13,9},{2,6},{6,2},{1... | collective-permute-start | bytes 1769480 | tf_op jit(solution)/shard_map/ppermute | solution.py:193
  56.7 19.4 %collective-permute-start.6 = (bf16[4,2,48,768]{3,2,1,0:T(8,128)(2,1)S(1)}, bf16[4,2,48,768]{3,2,1,0:T(8,128)(2,1)S(1)}, u32[]{:S(2)}, u32[]{:S(2)}) collective-permute-start(bf16[4,2,48,768]{3,2,1,0:T(8,128)(2,1)S(1)} %constant_dynamic-update-slice_fusion.refs_1_), channel_id=1, source_target_pairs={{0,4},{4,0},{8,12},{12,8},{1,5},{5,1},{9,13},{13,9},{2,6},{6,2},{1... | collective-permute-start | bytes 1769480 | tf_op jit(solution)/shard_map/ppermute | solution.py:193
  57.2 19.0 %collective-permute-start.7 = (bf16[4,2,48,768]{3,2,1,0:T(8,128)(2,1)}, bf16[4,2,48,768]{3,2,1,0:T(8,128)(2,1)}, u32[]{:S(2)}, u32[]{:S(2)}) collective-permute-start(bf16[4,2,48,768]{3,2,1,0:T(8,128)(2,1)} %collective-permute-done.4.refs_2_), channel_id=1, source_target_pairs={{0,4},{4,0},{8,12},{12,8},{1,5},{5,1},{9,13},{13,9},{2,6},{6,2},{1... | collective-permute-start | bytes 1769480 | tf_op jit(solution)/shard_map/ppermute | solution.py:193
  70.9 0.8 %copy-start.3 = (bf16[4,2,48,768]{3,2,1,0:T(8,128)(2,1)}, bf16[4,2,48,768]{3,2,1,0:T(8,128)(2,1)S(1)}, u32[]{:S(2)}) copy-start(bf16[4,2,48,768]{3,2,1,0:T(8,128)(2,1)S(1)} %collective-permute-done.5.refs_4_) | copy-start | bytes 1769476
  70.9 0.9 %copy-start = (bf16[16,48,256]{2,1,0:T(8,128)(2,1)}, bf16[16,48,256]{2,1,0:T(8,128)(2,1)S(1)}, u32[]{:S(2)}) copy-start(bf16[16,48,256]{2,1,0:T(8,128)(2,1)S(1)} %all-to-all-done.1) | copy-start | bytes 1179652
  70.9 5.3 %collective-permute-start.9 = (bf16[4,2,48,768]{3,2,1,0:T(8,128)(2,1)S(1)}, bf16[4,2,48,768]{3,2,1,0:T(8,128)(2,1)}, u32[]{:S(2)}, u32[]{:S(2)}) collective-permute-start(bf16[4,2,48,768]{3,2,1,0:T(8,128)(2,1)S(1)} %collective-permute-done.5.refs_4_), channel_id=1, source_target_pairs={{0,4},{4,0},{8,12},{12,8},{1,5},{5,1},{9,13},{13,9},{2,6},{6,2},{1... | collective-permute-start | bytes 1769480 | tf_op jit(solution)/shard_map/ppermute | solution.py:193
  76.2 0.8 %copy-start.4 = (bf16[4,2,48,768]{3,2,1,0:T(8,128)(2,1)}, bf16[4,2,48,768]{3,2,1,0:T(8,128)(2,1)S(1)}, u32[]{:S(2)}) copy-start(bf16[4,2,48,768]{3,2,1,0:T(8,128)(2,1)S(1)} %collective-permute-done.6.refs_2_) | copy-start | bytes 1769476
  76.2 1.0 %copy-start.2 = (bf16[4,2,48,768]{3,2,1,0:T(8,128)(2,1)}, bf16[4,2,48,768]{3,2,1,0:T(8,128)(2,1)S(1)}, u32[]{:S(2)}) copy-start(bf16[4,2,48,768]{3,2,1,0:T(8,128)(2,1)S(1)} %collective-permute-done.8.refs_4_) | copy-start | bytes 1769476

commit v2 on v1

--- a/solution.py
+++ b/solution.py
@@ -5,10 +5,12 @@
 from jax.experimental.pallas import tpu as pltpu
 from jax.sharding import PartitionSpec as P
 
+
 LANES = 128
 STEP = 8
 BUILD = 8
 CONV = 16
+CHUNK = 8
 
 
 def per_step(count, most):
@@ -20,7 +22,10 @@
     block = 16
     lane = lax.broadcasted_iota(jnp.int32, (block, LANES), 1) % width
     row = lax.broadcasted_iota(jnp.int32, (block, LANES), 0)
-    bands = [jnp.abs(row + start - lane) <= half for start in range(0, width, block)]
+    bands = [
+        jnp.where(jnp.abs(row + start - lane) <= half, 1.0, 0.0).astype(jnp.bfloat16)
+        for start in range(0, width, block)
+    ]
 
     def build(channel, carry):
         for shift in range(steps):
@@ -28,14 +33,12 @@
                 taps = v_ref[channel, shift, tile : tile + 1, :]
                 taps = jnp.broadcast_to(taps.astype(jnp.float32), (block, LANES))
                 turned = pltpu.roll(taps, LANES - half, axis=1, stride=1, stride_axis=0)
+                turned = turned.astype(jnp.bfloat16)
                 for index, band in enumerate(bands):
                     start = index * block
                     piece = turned if start == 0 else pltpu.roll(turned, start, axis=1)
-                    out_ref[
-                        channel,
-                        shift * width + start : shift * width + start + block,
-                        tile * LANES : (tile + 1) * LANES,
-                    ] = jnp.where(band, piece, 0.0).astype(jnp.bfloat16)
+                    low = shift * width + start
+                    out_ref[channel, tile, low : low + block, :] = piece * band
         return carry
 
     lax.fori_loop(0, count, build, 0)
@@ -43,7 +46,7 @@
 
 def conv_kernel(matrix_ref, img_ref, out_ref, shifted, *, half, segs):
     count, height, width = img_ref.shape
-    tiles = matrix_ref.shape[2] // LANES
+    tiles = matrix_ref.shape[1]
     rows = height + STEP * (tiles * segs - 1)
 
     @pl.when(pl.program_id(0) == 0)
@@ -63,7 +66,8 @@
             ],
             axis=1,
         )
-        product = jnp.dot(left, matrix_ref[channel], preferred_element_type=jnp.float32)
+        matrix = jnp.concatenate([matrix_ref[channel, t] for t in range(tiles)], axis=1)
+        product = jnp.dot(left, matrix, preferred_element_type=jnp.float32)
         keep = height + STEP * (segs - 1)
         total = product[:keep, :LANES]
         for tile in range(1, tiles):
@@ -76,6 +80,138 @@
         out_ref[channel] = (x + mixed).astype(out_ref.dtype)
 
 
+def moved_kernel(
+    recv_ref, into_ref, back_ref, matrix_hbm, out_ref, shifted, result, matrices, sems, *, half, segs
+):
+    count = recv_ref.shape[1]
+    across = into_ref.shape[0] // LANES
+    parts = recv_ref.shape[2] // LANES
+    down = recv_ref.shape[0] // across
+    chunks, chunk, tiles = matrices.shape[:3]
+    width = LANES // segs
+    taken = into_ref.shape[1] // LANES
+    height = down * parts * taken
+    pitch = shifted.shape[0] // count
+    rows = height + STEP * (tiles * segs - 1)
+    copies = [
+        pltpu.make_async_copy(
+            matrix_hbm.at[pl.ds(index * chunk, chunk)], matrices.at[index], sems.at[index]
+        )
+        for index in range(chunks)
+    ]
+    for copy in copies:
+        copy.start()
+    shifted[...] = jnp.zeros_like(shifted)
+    left = jnp.concatenate(
+        [
+            jnp.concatenate(
+                [
+                    recv_ref[r * across + c, :, part * LANES : (part + 1) * LANES]
+                    for c in range(across)
+                ],
+                axis=1,
+            )
+            for r in range(down)
+            for part in range(parts)
+        ],
+        axis=0,
+    )
+    images = jnp.dot(left, into_ref[...], preferred_element_type=jnp.float32)
+    for group in range(down * parts):
+        for step in range(taken):
+            row = half + group * taken + step
+            shifted[pl.ds(row, count, stride=pitch), :] = images[
+                group * count : (group + 1) * count, step * LANES : (step + 1) * LANES
+            ]
+    first = lax.broadcasted_iota(jnp.int32, (rows, LANES), 1) // width
+    for channel in range(count):
+        if channel % chunk == 0:
+            copies[channel // chunk].wait()
+        base = channel * pitch
+        pieces = []
+        for shift in range(0, STEP, segs):
+            piece = shifted[base + shift : base + shift + rows, :]
+            for seg in range(1, segs):
+                low = base + shift + seg
+                piece = jnp.where(first == seg, shifted[low : low + rows, :], piece)
+            pieces.append(piece.astype(jnp.bfloat16))
+        matrix = [matrices[channel // chunk, channel % chunk, tile] for tile in range(tiles)]
+        product = jnp.dot(
+            jnp.concatenate(pieces, axis=1),
+            jnp.concatenate(matrix, axis=1),
+            preferred_element_type=jnp.float32,
+        )
+        keep = height + STEP * (segs - 1)
+        total = product[:keep, :LANES]
+        for tile in range(1, tiles):
+            start = tile * segs * STEP
+            total = total + product[start : start + keep, tile * LANES : (tile + 1) * LANES]
+        mixed = total[:height, :]
+        for seg in range(1, segs):
+            part = total[seg * STEP : seg * STEP + height, :]
+            mixed = mixed + pltpu.roll(part, LANES - seg * width, axis=1)
+        x = shifted[base + half : base + half + height, :]
+        result[channel * height : (channel + 1) * height, :] = x + mixed
+    left = jnp.concatenate(
+        [
+            jnp.concatenate(
+                [
+                    result[pl.ds(group * taken + step, count, stride=height), :].astype(
+                        jnp.bfloat16
+                    )
+                    for step in range(taken)
+                ],
+                axis=1,
+            )
+            for group in range(down * parts)
+        ],
+        axis=0,
+    )
+    moved = jnp.dot(left, back_ref[...], preferred_element_type=jnp.float32)
+    for r in range(down):
+        for part in range(parts):
+            group = r * parts + part
+            for c in range(across):
+                out_ref[r * across + c, :, part * LANES : (part + 1) * LANES] = moved[
+                    group * count : (group + 1) * count, c * LANES : (c + 1) * LANES
+                ].astype(out_ref.dtype)
+
+
+def moves_of(across, tile_cols):
+    taken = LANES // tile_cols
+    width = across * tile_cols
+    lane = jnp.arange(across * LANES)
+    step, col = lane % LANES // tile_cols, lane // LANES * tile_cols + lane % tile_cols
+    cell = jnp.arange(taken * LANES)
+    same = step[:, None] == (cell // LANES)[None, :]
+    into = same & (col[:, None] == (cell % LANES % width)[None, :])
+    back = same & (col[:, None] == (cell % LANES)[None, :])
+    return into.astype(jnp.bfloat16), back.T.astype(jnp.bfloat16)
+
+
+def spread_moved(matrices, moves, received, half, across, tile_cols):
+    devices, count, cells = received.shape
+    segs = LANES // (across * tile_cols)
+    height = devices // across * cells // tile_cols
+    tiles = matrices.shape[1]
+    pitch = height + STEP * tiles * segs
+    chunk = per_step(count, CHUNK)
+    whole = pl.BlockSpec(memory_space=pltpu.VMEM)
+    return pl.pallas_call(
+        lambda *refs: moved_kernel(*refs, half=half, segs=segs),
+        in_specs=[whole] * 3 + [pl.BlockSpec(memory_space=pl.ANY)],
+        out_specs=whole,
+        out_shape=jax.ShapeDtypeStruct(received.shape, received.dtype),
+        scratch_shapes=[
+            pltpu.VMEM((count * pitch, LANES), jnp.float32),
+            pltpu.VMEM((count * height, LANES), jnp.float32),
+            pltpu.VMEM((count // chunk, chunk) + matrices.shape[1:], matrices.dtype),
+            pltpu.SemaphoreType.DMA((count // chunk,)),
+        ],
+        name="depthwise_moved",
+    )(received, *moves, matrices)
+
+
 def matrices_of(taps, width):
     side, _, count = taps.shape
     half = (side - 1) // 2
@@ -86,17 +222,17 @@
     v = v.reshape(count, groups, STEP, width).transpose(0, 2, 1, 3)
     v = v.reshape(count, STEP, groups // segs, LANES)
     several = per_step(count, BUILD)
-    shape = (STEP * width, groups * width)
+    shape = (groups // segs, STEP * width, LANES)
     return pl.pallas_call(
         lambda *refs: toeplitz_kernel(*refs, half=half, width=width),
         grid=(count // several,),
         in_specs=[pl.BlockSpec((several,) + v.shape[1:], lambda i: (i, 0, 0, 0))],
-        out_specs=pl.BlockSpec((several,) + shape, lambda i: (i, 0, 0)),
+        out_specs=pl.BlockSpec((several,) + shape, lambda i: (i, 0, 0, 0)),
         out_shape=jax.ShapeDtypeStruct((count,) + shape, taps.dtype),
         cost_estimate=pl.CostEstimate(
-            flops=count * shape[0] * shape[1] * 4,
+            flops=count * groups * STEP * width * width * 4,
             transcendentals=0,
-            bytes_accessed=count * shape[0] * shape[1] * 2,
+            bytes_accessed=count * groups * STEP * width * width * 2,
         ),
         name="toeplitz",
     )(v)
@@ -105,13 +241,13 @@
 def spread_of(matrices, images, half):
     count, height, width = images.shape
     segs = LANES // width
-    groups = matrices.shape[2] // width
+    groups = matrices.shape[1] * segs
     several = per_step(count, CONV)
     return pl.pallas_call(
         lambda *refs: conv_kernel(*refs, half=half, segs=segs),
         grid=(count // several,),
         in_specs=[
-            pl.BlockSpec((several,) + matrices.shape[1:], lambda i: (i, 0, 0)),
+            pl.BlockSpec((several,) + matrices.shape[1:], lambda i: (i, 0, 0, 0)),
             pl.BlockSpec((several, height, width), lambda i: (i, 0, 0)),
         ],
         out_specs=pl.BlockSpec((several, height, width), lambda i: (i, 0, 0)),
@@ -193,15 +329,16 @@
     return lax.ppermute(array, axis, [(i, i ^ 1) for i in range(size)])
 
 
-def on_device(features, dw_kernel, w_up, w_down):
+def on_tile(features, dw_kernel, w_up, w_down):
     axes = ("rows", "cols")
     down = lax.axis_size("rows")
     across = lax.axis_size("cols")
+    pages = lax.axis_size("pages")
     devices = down * across
     tile_rows, tile_cols, channels = features.shape
     cells = tile_rows * tile_cols
     own = channels // devices
-    pages = lax.axis_size("pages")
+    half = (dw_kernel.shape[0] - 1) // 2
     units = w_up.shape[1] // pages
     piece = jnp.stack([w_up.T, w_down.T])[None]
     piece = lax.dynamic_slice_in_dim(piece, lax.axis_index("pages") * units, units, axis=2)
@@ -209,19 +346,23 @@
     turned = features.reshape(cells, channels).T.reshape(devices, own, cells)
     images = lax.all_to_all(turned, axes, 0, 0, tiled=True)
     matrices = matrices_of(dw_kernel, across * tile_cols)
-    images, matrices, line = lax.optimization_barrier((images, matrices, line))
+    moves = moves_of(across, tile_cols)
+    images, matrices, moves, line = lax.optimization_barrier((images, matrices, moves, line))
     line = jnp.concatenate(line, axis=0)
     others = [turn(line, "rows", shift, 2) for shift in range(1, down // 2)]
     near = [line] + [turn(line, "pages", shift) for shift in range(1, pages)]
-    images = images.reshape(down, across, own, tile_rows, tile_cols)
-    images = images.transpose(2, 0, 3, 1, 4).reshape(own, down * tile_rows, across * tile_cols)
-    spread = spread_of(matrices, images, (dw_kernel.shape[0] - 1) // 2)
-    spread = spread.reshape(own, down, tile_rows, across, tile_cols)
-    spread = spread.transpose(1, 3, 0, 2, 4).reshape(devices, own, cells)
-    spread, others, near = lax.optimization_barrier((spread, others, near))
+    if own % 16 == 0:
+        spread = spread_moved(matrices, moves, images, half, across, tile_cols)
+    else:
+        images = images.reshape(down, across, own, tile_rows, tile_cols)
+        images = images.transpose(2, 0, 3, 1, 4)
+        images = images.reshape(own, down * tile_rows, across * tile_cols)
+        spread = spread_of(matrices, images, half)
+        spread = spread.reshape(own, down, tile_rows, across, tile_cols)
+        spread = spread.transpose(1, 3, 0, 2, 4).reshape(devices, own, cells)
+    last = [turn(other, "pages", shift) for other in others for shift in range(1, pages)]
     near = near + others
     far = [partner(each, "rows") for each in near]
-    last = [turn(other, "pages", shift) for other in others for shift in range(1, pages)]
     spread = lax.all_to_all(spread, axes, 0, 0, tiled=True)
     spread, last = lax.optimization_barrier((spread, last))
     far += [partner(each, "rows") for each in last]
@@ -231,7 +372,7 @@
 
 def solution(mesh):
     return jax.shard_map(
-        on_device,
+        on_tile,
         mesh=mesh,
         in_specs=(
             P(("pages", "rows"), "cols", None),

time: 81.8 us -> 84.9 us (1.038)
  waiting for transfers between devices: 15.3 us -> 25.7 us
  local copies, waits for them, and re-layouts: 12.5 us -> 5.37 us
  starting transfers between devices: 25 us -> 20.5 us
  other arithmetic: 0.94 us -> 3.97 us
  Pallas kernels: 27.3 us -> 28.7 us
    ppermute x6, waiting for transfers between devices: 15.3 us -> 25.7 us  [turn(): lax.ppermute(array, axis, [(i, (i + shift * within) % size) for i in rang...]
    all_to_all x2, starting transfers between devices: 14 us -> 9.79 us  [the longest x1 5.12 us: on_tile(): images = lax.all_to_all(turned, axes, 0, 0, tiled=True)]
    convert_element_type x0 -> x2, other arithmetic: none -> 2.98 us  [moves_of(): return (into.astype(jnp.bfloat16), back.T.astype(jnp.bfloat16))]
    transpose x3 -> x0, local copies, waits for them, and re-layouts: 2.47 us -> none  [the longest x1 1.91 us: on_device(): turned = features.reshape(cells, channels).T.reshape(devices, own, cells)]
    pallas_call x1 -> x0, local copies, waits for them, and re-layouts: 1.93 us -> none  [spread_of(): pl.pallas_call(lambda *refs: conv_kernel(*refs, half=half, segs=segs), gr...]
    optimization_barrier x2 -> x0, local copies, waits for them, and re-layouts: 1.55 us -> none  [the longest x1 1.07 us: on_device(): spread, others, near = lax.optimization_barrier((spread, others, near))]
    pallas_call x1, Pallas kernels: 7.27 us -> 8.66 us  [spread_moved(): pl.pallas_call(lambda *refs: moved_kernel(*refs, half=half, segs=segs), i...]
    rev x1, local copies, waits for them, and re-layouts: 1.12 us -> 0.2 us  [matrices_of(): v = jnp.transpose(taps[:, ::-1, :], (2, 0, 1))]
  transfers between devices with their start and end apart: 12 -> 12, of which waited for: 3 -> 2; matrix products, arithmetic and copies ran while one was open for 11% -> 8% of each run, Pallas kernels for 29% -> 29%
where the time goes in v2:
time: 84.9 us; the launch traced here: 84.4 us
  Pallas kernels  28.7 us (34%)
  waiting for transfers between devices  25.7 us (30%)
  starting transfers between devices  20.5 us (24%)
  local copies, waits for them, and re-layouts  5.37 us (6%)
  other arithmetic  3.97 us (5%)
    ppermute x6, waiting for transfers between devices, turn(): lax.ppermute(array, axis, [(i, (i + shift * within) % size) for i in rang...  25.7 us
    pallas_call x1, Pallas kernels, matrices_of(): pl.pallas_call(lambda *refs: toeplitz_kernel(*refs, half=half, width=widt...  11.7 us
    ppermute x6, starting transfers between devices, turn(): lax.ppermute(array, axis, [(i, (i + shift * within) % size) for i in rang...  10.2 us
    pallas_call x1, Pallas kernels, spread_moved(): pl.pallas_call(lambda *refs: moved_kernel(*refs, half=half, segs=segs), i...  8.66 us
    all_to_all x1, starting transfers between devices, on_tile(): images = lax.all_to_all(turned, axes, 0, 0, tiled=True)  5.12 us
    all_to_all x1, starting transfers between devices, on_tile(): spread = lax.all_to_all(spread, axes, 0, 0, tiled=True)  4.67 us
    pallas_call x1, Pallas kernels, block_of(): pl.pallas_call(first_kernel, in_specs=[whole] * (1 + len(near)), out_spec...  4.29 us
    pallas_call x1, Pallas kernels, block_of(): pl.pallas_call(second_kernel, in_specs=[whole] * (2 + len(far)), out_spec...  4.06 us
  transfers between devices with their start and end apart: 12, of which 2 were waited for; matrix products, arithmetic and copies ran while one was open for 8% of the time, Pallas kernels for 29%

profile of v2, /device:TPU:0, one launch (start us, length us, event | category | flops | bytes accessed | tf_op | source)
XLA Modules:
  0.0 84.4 jit_solution(8753427244273602845)
XLA Ops:
  0.0 1.0 %fusion.1 = bf16[1,2,48,768]{3,2,1,0:T(8,128)(2,1)S(1)} fusion(s32[]{:T(128)S(6)} %select_n.89, bf16[1,96,768]{2,1,0:T(8,128)(2,1)} %bitcast.22, bf16[1,96,768]{2,1,0:T(8,128)(2,1)} %bitcast.23), kind=kLoop, calls=%fused_computation.5 | loop fusion | flops 294912 | bytes 442372 | tf_op jit(solution)/shard_map/dynamic_slice | solution.py:344
  1.0 5.1 %collective-permute-start.2 = (bf16[1,2,48,768]{3,2,1,0:T(8,128)(2,1)S(1)}, bf16[1,2,48,768]{3,2,1,0:T(8,128)(2,1)S(1)}, u32[]{:S(2)}, u32[]{:S(2)}) collective-permute-start(bf16[1,2,48,768]{3,2,1,0:T(8,128)(2,1)S(1)} %fusion.1), channel_id=1, source_target_pairs={{0,3},{1,0},{2,1},{3,2},{4,7},{5,4},{6,5},{7,6},{8,11},{9,8},{10,9... | collective-permute-start | bytes 442376 | tf_op jit(solution)/shard_map/ppermute | solution.py:322
  6.1 1.0 %collective-permute-start = (bf16[1,2,48,768]{3,2,1,0:T(8,128)(2,1)S(1)}, bf16[1,2,48,768]{3,2,1,0:T(8,128)(2,1)S(1)}, u32[]{:S(2)}, u32[]{:S(2)}) collective-permute-start(bf16[1,2,48,768]{3,2,1,0:T(8,128)(2,1)S(1)} %fusion.1), channel_id=1, source_target_pairs={{0,1},{1,2},{2,3},{3,0},{4,5},{5,6},{6,7},{7,4},{8,9},{9,10},{10,1... | collective-permute-start | bytes 442376 | tf_op jit(solution)/shard_map/ppermute | solution.py:322
  7.1 1.9 %copy.5 = bf16[256,768]{0,1:T(8,128)(2,1)} copy(bf16[256,768]{1,0:T(8,128)(2,1)} %bitcast.21) | data formatting | bytes 786432 | tf_op jit(solution)/shard_map/reshape | solution.py:346
  9.0 5.1 %all-to-all-start = ((bf16[16,48,256]{2,1,0:T(8,128)(2,1)}), bf16[16,48,256]{2,1,0:T(8,128)(2,1)S(1)}, u32[]{:S(2)}, u32[]{:S(2)}) async-start(bf16[16,48,256]{2,1,0:T(8,128)(2,1)} %bitcast.2), calls=%async_computation | async-start | bytes 786432 | tf_op jit(solution)/shard_map/all_to_all | solution.py:347
  14.2 0.2 rev.3
  14.4 0.1 pad.4
  14.5 0.6 copy.6
  15.1 0.9 %reshape.103.refs_0_ = bf16[48,8,2,128]{3,2,1,0:T(2,128)(2,1)} reshape(bf16[48,8,4,64]{3,2,1,0:T(4,128)(2,1)S(1)} %bitcast.18) | data formatting | bytes 393216 | tf_op jit(solution)/shard_map/reshape | solution.py:223
  16.0 11.7 %toeplitz.1.refs_3_ = bf16[48,2,512,128]{3,2,1,0:T(8,128)(2,1)} custom-call(bf16[48,8,2,128]{3,2,1,0:T(2,128)(2,1)} %reshape.103.refs_0_), custom_call_target="tpu_custom_call" | custom-call | flops 25165824 | bytes 12582912 | tf_op jit(solution)/shard_map/toeplitz/pallas_call | solution.py:226
  27.7 1.4 %and_convert_fusion.1.refs_1_ = bf16[512,1024]{1,0:T(8,128)(2,1)} fusion(s32[1024]{0:T(1024)S(1)} %get-tuple-element.29, s32[1024]{0:T(1024)S(1)} %get-tuple-element.30, s32[512]{0:T(512)S(1)} %get-tuple-element.32, s32[512]{0:T(512)S(1)} %get-tuple-element.31), kind=kLoop, calls=%fused_computation.1 | loop fusion | flops 2097152 | bytes 1060864 | tf_op jit(solution)/shard_map/convert_element_type | solution.py:189
  29.1 1.6 %and_convert_fusion.refs_2_ = bf16[1024,512]{1,0:T(8,128)(2,1)} fusion(s32[512]{0:T(512)S(1)} %get-tuple-element.32, s32[512]{0:T(512)S(1)} %get-tuple-element.31, s32[1024]{0:T(1024)S(1)} %fusion.2, s32[1024]{0:T(1024)S(1)} %get-tuple-element.30), kind=kLoop, calls=%fused_computation | loop fusion | flops 2097152 | bytes 1060864 | tf_op jit(solution)/shard_map/convert_element_type | solution.py:189
  30.8 2.0 %collective-permute-start.3 = (bf16[4,2,48,768]{3,2,1,0:T(8,128)(2,1)S(1)}, bf16[4,2,48,768]{3,2,1,0:T(8,128)(2,1)S(1)}, u32[]{:S(2)}, u32[]{:S(2)}) collective-permute-start(bf16[4,2,48,768]{3,2,1,0:T(8,128)(2,1)S(1)} %constant_dynamic-update-slice_fusion.refs_1_), channel_id=1, source_target_pairs={{0,8},{4,12},{8,0},{12,4},{1,9},{5,13},{9,1},{13,5},{2,10},{6,14},... | collective-permute-start | bytes 1769480 | tf_op jit(solution)/shard_map/ppermute | solution.py:322
  32.8 8.7 %depthwise_moved.1 = bf16[16,48,256]{2,1,0:T(8,128)(2,1)} custom-call(bf16[16,48,256]{2,1,0:T(8,128)(2,1)} %copy-done.1, bf16[512,1024]{1,0:T(8,128)(2,1)} %and_convert_fusion.1.refs_1_, bf16[1024,512]{1,0:T(8,128)(2,1)} %and_convert_fusion.refs_2_, bf16[48,2,512,128]{3,2,1,0:T(8,128)(2,1)} %toeplitz.1.refs_3_), custom_call_target="tpu_custom_call" | custom-call | tf_op jit(solution)/shard_map/depthwise_moved/pallas_call | solution.py:200
  41.4 4.7 %all-to-all-start.1 = ((bf16[16,48,256]{2,1,0:T(8,128)(2,1)}), bf16[16,48,256]{2,1,0:T(8,128)(2,1)S(1)}, u32[]{:S(2)}, u32[]{:S(2)}) async-start(bf16[16,48,256]{2,1,0:T(8,128)(2,1)} %depthwise_moved.1), calls=%async_computation.1 | async-start | bytes 786432 | tf_op jit(solution)/shard_map/all_to_all | solution.py:366
  46.1 1.6 %collective-permute-start.5 = (bf16[4,2,48,768]{3,2,1,0:T(8,128)(2,1)S(1)}, bf16[4,2,48,768]{3,2,1,0:T(8,128)(2,1)S(1)}, u32[]{:S(2)}, u32[]{:S(2)}) collective-permute-start(bf16[4,2,48,768]{3,2,1,0:T(8,128)(2,1)S(1)} %constant_dynamic-update-slice_fusion.refs_1_), channel_id=1, source_target_pairs={{0,16},{16,0},{1,17},{17,1},{2,18},{18,2},{3,19},{19,3},{4,20},{20... | collective-permute-start | bytes 1769480 | tf_op jit(solution)/shard_map/ppermute | solution.py:322
  47.7 0.5 collective-permute-start.4
  48.2 0.5 collective-permute-start.8
  48.7 13.7 %collective-permute-done.5.refs_2_ = bf16[4,2,48,768]{3,2,1,0:T(8,128)(2,1)S(1)} collective-permute-done((bf16[4,2,48,768]{3,2,1,0:T(8,128)(2,1)S(1)}, bf16[4,2,48,768]{3,2,1,0:T(8,128)(2,1)S(1)}, u32[]{:S(2)}, u32[]{:S(2)}) %collective-permute-start.5) | collective-permute-done | bytes 589856 | tf_op jit(solution)/shard_map/ppermute | solution.py:322
  62.4 12.0 %collective-permute-done.4.refs_4_ = bf16[4,2,48,768]{3,2,1,0:T(8,128)(2,1)S(1)} collective-permute-done((bf16[4,2,48,768]{3,2,1,0:T(8,128)(2,1)S(1)}, bf16[4,2,48,768]{3,2,1,0:T(8,128)(2,1)S(1)}, u32[]{:S(2)}, u32[]{:S(2)}) %collective-permute-start.4) | collective-permute-done | bytes 589856 | tf_op jit(solution)/shard_map/ppermute | solution.py:322
  74.4 0.8 copy-done.5
  75.2 4.3 %feed_forward_near.1 = (bf16[256,768]{1,0:T(8,128)(2,1)}, f32[256,768]{1,0:T(8,128)}) custom-call(bf16[768,256]{1,0:T(8,128)(2,1)} %bitcast.19, bf16[4,2,48,768]{3,2,1,0:T(8,128)(2,1)} %copy-done.2, bf16[4,2,48,768]{3,2,1,0:T(8,128)(2,1)} %copy-done.6, bf16[4,2,48,768]{3,2,1,0:T(8,128)(2,1)} %copy-done.3, bf16[4,2,48,768]{3,2,1,0:T(8,128)(2,1)} %copy-done.5), custom_call_target="tpu_custom_call" | custom-call | tf_op jit(solution)/shard_map/feed_forward_near/pallas_call | solution.py:301
  79.6 0.8 copy-done.4
  80.3 4.1 %feed_forward_far.1 = bf16[256,768]{1,0:T(8,128)(2,1)} custom-call(bf16[256,768]{1,0:T(8,128)(2,1)} %get-tuple-element.27.refs_0_, f32[256,768]{1,0:T(8,128)} %get-tuple-element.28.refs_1_, bf16[4,2,48,768]{3,2,1,0:T(8,128)(2,1)} %copy-done.4, bf16[4,2,48,768]{3,2,1,0:T(8,128)(2,1)} %collective-permute-done.7.refs_3_, ...), custom_call_target="tpu_custom_call" | custom-call | tf_op jit(solution)/shard_map/feed_forward_far/pallas_call | solution.py:311
  (35 shorter events, 0.1 us)
Async XLA Ops:
  0.0 14.2 %copy-start.7 = (bf16[31,31,48]{2,1,0:T(8,128)(2,1)S(1)}, bf16[31,31,48]{2,1,0:T(8,128)(2,1)}, u32[]{:S(2)}) copy-start(bf16[31,31,48]{2,1,0:T(8,128)(2,1)} %param.5) | copy-start | bytes 276772
  1.0 29.7 %collective-permute-start.2 = (bf16[1,2,48,768]{3,2,1,0:T(8,128)(2,1)S(1)}, bf16[1,2,48,768]{3,2,1,0:T(8,128)(2,1)S(1)}, u32[]{:S(2)}, u32[]{:S(2)}) collective-permute-start(bf16[1,2,48,768]{3,2,1,0:T(8,128)(2,1)S(1)} %fusion.1), channel_id=1, source_target_pairs={{0,3},{1,0},{2,1},{3,2},{4,7},{5,4},{6,5},{7,6},{8,11},{9,8},{10,9... | collective-permute-start | bytes 442376 | tf_op jit(solution)/shard_map/ppermute | solution.py:322
  6.1 24.6 %collective-permute-start.1 = (bf16[1,2,48,768]{3,2,1,0:T(8,128)(2,1)S(1)}, bf16[1,2,48,768]{3,2,1,0:T(8,128)(2,1)S(1)}, u32[]{:S(2)}, u32[]{:S(2)}) collective-permute-start(bf16[1,2,48,768]{3,2,1,0:T(8,128)(2,1)S(1)} %fusion.1), channel_id=1, source_target_pairs={{0,2},{1,3},{2,0},{3,1},{4,6},{5,7},{6,4},{7,5},{8,10},{9,11},{10,... | collective-permute-start | bytes 442376 | tf_op jit(solution)/shard_map/ppermute | solution.py:322
  6.1 24.6 %collective-permute-start = (bf16[1,2,48,768]{3,2,1,0:T(8,128)(2,1)S(1)}, bf16[1,2,48,768]{3,2,1,0:T(8,128)(2,1)S(1)}, u32[]{:S(2)}, u32[]{:S(2)}) collective-permute-start(bf16[1,2,48,768]{3,2,1,0:T(8,128)(2,1)S(1)} %fusion.1), channel_id=1, source_target_pairs={{0,1},{1,2},{2,3},{3,0},{4,5},{5,6},{6,7},{7,4},{8,9},{9,10},{10,1... | collective-permute-start | bytes 442376 | tf_op jit(solution)/shard_map/ppermute | solution.py:322
  9.0 21.6 %all-to-all-start = ((bf16[16,48,256]{2,1,0:T(8,128)(2,1)}), bf16[16,48,256]{2,1,0:T(8,128)(2,1)S(1)}, u32[]{:S(2)}, u32[]{:S(2)}) async-start(bf16[16,48,256]{2,1,0:T(8,128)(2,1)} %bitcast.2), calls=%async_computation | async-start | bytes 786432 | tf_op jit(solution)/shard_map/all_to_all | solution.py:347
  30.7 2.1 %copy-start.1 = (bf16[16,48,256]{2,1,0:T(8,128)(2,1)}, bf16[16,48,256]{2,1,0:T(8,128)(2,1)S(1)}, u32[]{:S(2)}) copy-start(bf16[16,48,256]{2,1,0:T(8,128)(2,1)S(1)} %all-to-all-done.refs_0_) | copy-start | bytes 1179652
  30.8 17.4 %copy-start.2 = (bf16[4,2,48,768]{3,2,1,0:T(8,128)(2,1)}, bf16[4,2,48,768]{3,2,1,0:T(8,128)(2,1)S(1)}, u32[]{:S(2)}) copy-start(bf16[4,2,48,768]{3,2,1,0:T(8,128)(2,1)S(1)} %constant_dynamic-update-slice_fusion.refs_1_) | copy-start | bytes 1769476
  30.8 16.9 %collective-permute-start.3 = (bf16[4,2,48,768]{3,2,1,0:T(8,128)(2,1)S(1)}, bf16[4,2,48,768]{3,2,1,0:T(8,128)(2,1)S(1)}, u32[]{:S(2)}, u32[]{:S(2)}) collective-permute-start(bf16[4,2,48,768]{3,2,1,0:T(8,128)(2,1)S(1)} %constant_dynamic-update-slice_fusion.refs_1_), channel_id=1, source_target_pairs={{0,8},{4,12},{8,0},{12,4},{1,9},{5,13},{9,1},{13,5},{2,10},{6,14},... | collective-permute-start | bytes 1769480 | tf_op jit(solution)/shard_map/ppermute | solution.py:322
  41.4 21.0 %all-to-all-start.1 = ((bf16[16,48,256]{2,1,0:T(8,128)(2,1)}), bf16[16,48,256]{2,1,0:T(8,128)(2,1)S(1)}, u32[]{:S(2)}, u32[]{:S(2)}) async-start(bf16[16,48,256]{2,1,0:T(8,128)(2,1)} %depthwise_moved.1), calls=%async_computation.1 | async-start | bytes 786432 | tf_op jit(solution)/shard_map/all_to_all | solution.py:366
  46.1 16.3 %collective-permute-start.5 = (bf16[4,2,48,768]{3,2,1,0:T(8,128)(2,1)S(1)}, bf16[4,2,48,768]{3,2,1,0:T(8,128)(2,1)S(1)}, u32[]{:S(2)}, u32[]{:S(2)}) collective-permute-start(bf16[4,2,48,768]{3,2,1,0:T(8,128)(2,1)S(1)} %constant_dynamic-update-slice_fusion.refs_1_), channel_id=1, source_target_pairs={{0,16},{16,0},{1,17},{17,1},{2,18},{18,2},{3,19},{19,3},{4,20},{20... | collective-permute-start | bytes 1769480 | tf_op jit(solution)/shard_map/ppermute | solution.py:322
  47.7 26.7 %copy-start.3 = (bf16[4,2,48,768]{3,2,1,0:T(8,128)(2,1)}, bf16[4,2,48,768]{3,2,1,0:T(8,128)(2,1)S(1)}, u32[]{:S(2)}) copy-start(bf16[4,2,48,768]{3,2,1,0:T(8,128)(2,1)S(1)} %collective-permute-done.3.refs_3_) | copy-start | bytes 1769476
  47.7 26.7 %collective-permute-start.4 = (bf16[4,2,48,768]{3,2,1,0:T(8,128)(2,1)S(1)}, bf16[4,2,48,768]{3,2,1,0:T(8,128)(2,1)S(1)}, u32[]{:S(2)}, u32[]{:S(2)}) collective-permute-start(bf16[4,2,48,768]{3,2,1,0:T(8,128)(2,1)S(1)} %collective-permute-done.3.refs_3_), channel_id=1, source_target_pairs={{0,16},{16,0},{1,17},{17,1},{2,18},{18,2},{3,19},{19,3},{4,20},{20... | collective-permute-start | bytes 1769480 | tf_op jit(solution)/shard_map/ppermute | solution.py:322
  48.2 31.3 %collective-permute-start.6 = (bf16[4,2,48,768]{3,2,1,0:T(8,128)(2,1)S(1)}, bf16[4,2,48,768]{3,2,1,0:T(8,128)(2,1)S(1)}, u32[]{:S(2)}, u32[]{:S(2)}) collective-permute-start(bf16[4,2,48,768]{3,2,1,0:T(8,128)(2,1)S(1)} %constant_dynamic-update-slice_fusion.refs_1_), channel_id=1, source_target_pairs={{0,4},{4,0},{8,12},{12,8},{1,5},{5,1},{9,13},{13,9},{2,6},{6,2},{1... | collective-permute-start | bytes 1769480 | tf_op jit(solution)/shard_map/ppermute | solution.py:329
  48.2 31.3 %collective-permute-start.8 = (bf16[4,2,48,768]{3,2,1,0:T(8,128)(2,1)S(1)}, bf16[4,2,48,768]{3,2,1,0:T(8,128)(2,1)}, u32[]{:S(2)}, u32[]{:S(2)}) collective-permute-start(bf16[4,2,48,768]{3,2,1,0:T(8,128)(2,1)S(1)} %collective-permute-done.3.refs_3_), channel_id=1, source_target_pairs={{0,4},{4,0},{8,12},{12,8},{1,5},{5,1},{9,13},{13,9},{2,6},{6,2},{1... | collective-permute-start | bytes 1769480 | tf_op jit(solution)/shard_map/ppermute | solution.py:329
  62.4 12.0 %copy-start.6 = (bf16[4,2,48,768]{3,2,1,0:T(8,128)(2,1)}, bf16[4,2,48,768]{3,2,1,0:T(8,128)(2,1)S(1)}, u32[]{:S(2)}) copy-start(bf16[4,2,48,768]{3,2,1,0:T(8,128)(2,1)S(1)} %collective-permute-done.5.refs_2_) | copy-start | bytes 1769476
  62.4 17.1 %collective-permute-start.7 = (bf16[4,2,48,768]{3,2,1,0:T(8,128)(2,1)S(1)}, bf16[4,2,48,768]{3,2,1,0:T(8,128)(2,1)}, u32[]{:S(2)}, u32[]{:S(2)}) collective-permute-start(bf16[4,2,48,768]{3,2,1,0:T(8,128)(2,1)S(1)} %collective-permute-done.5.refs_2_), channel_id=1, source_target_pairs={{0,4},{4,0},{8,12},{12,8},{1,5},{5,1},{9,13},{13,9},{2,6},{6,2},{1... | collective-permute-start | bytes 1769480 | tf_op jit(solution)/shard_map/ppermute | solution.py:329
  62.4 12.0 %copy-start = (bf16[16,48,256]{2,1,0:T(8,128)(2,1)}, bf16[16,48,256]{2,1,0:T(8,128)(2,1)S(1)}, u32[]{:S(2)}) copy-start(bf16[16,48,256]{2,1,0:T(8,128)(2,1)S(1)} %all-to-all-done.1) | copy-start | bytes 1179652
  74.4 0.8 copy-start.5
  74.4 5.1 %collective-permute-start.9 = (bf16[4,2,48,768]{3,2,1,0:T(8,128)(2,1)S(1)}, bf16[4,2,48,768]{3,2,1,0:T(8,128)(2,1)}, u32[]{:S(2)}, u32[]{:S(2)}) collective-permute-start(bf16[4,2,48,768]{3,2,1,0:T(8,128)(2,1)S(1)} %collective-permute-done.4.refs_4_), channel_id=1, source_target_pairs={{0,4},{4,0},{8,12},{12,8},{1,5},{5,1},{9,13},{13,9},{2,6},{6,2},{1... | collective-permute-start | bytes 1769480 | tf_op jit(solution)/shard_map/ppermute | solution.py:329
  79.5 0.8 copy-start.4

commit v3 on v2

--- a/solution.py
+++ b/solution.py
@@ -1,5 +1,6 @@
 import jax
 import jax.numpy as jnp
+import numpy as np
 from jax import lax
 from jax.experimental import pallas as pl
 from jax.experimental.pallas import tpu as pltpu
@@ -41,7 +42,7 @@
                     out_ref[channel, tile, low : low + block, :] = piece * band
         return carry
 
-    lax.fori_loop(0, count, build, 0)
+    lax.fori_loop(0, count, build, 0, unroll=per_step(count, 2))
 
 
 def conv_kernel(matrix_ref, img_ref, out_ref, shifted, *, half, segs):
@@ -80,24 +81,27 @@
         out_ref[channel] = (x + mixed).astype(out_ref.dtype)
 
 
-def moved_kernel(
-    recv_ref, into_ref, back_ref, matrix_hbm, out_ref, shifted, result, matrices, sems, *, half, segs
-):
+def moved_kernel(*refs, half, segs):
+    recv_ref, move_ref, *matrix_hbms = refs[:-5]
+    out_ref, shifted, result, matrices, sems = refs[-5:]
     count = recv_ref.shape[1]
-    across = into_ref.shape[0] // LANES
+    across = move_ref.shape[0] // LANES
     parts = recv_ref.shape[2] // LANES
     down = recv_ref.shape[0] // across
-    chunks, chunk, tiles = matrices.shape[:3]
+    _, chunk, tiles = matrices.shape[:3]
     width = LANES // segs
-    taken = into_ref.shape[1] // LANES
+    taken = move_ref.shape[1] // width
     height = down * parts * taken
     pitch = shifted.shape[0] // count
     rows = height + STEP * (tiles * segs - 1)
+    sources = [
+        matrix_hbm.at[pl.ds(start, chunk)]
+        for matrix_hbm in matrix_hbms
+        for start in range(0, matrix_hbm.shape[0], chunk)
+    ]
     copies = [
-        pltpu.make_async_copy(
-            matrix_hbm.at[pl.ds(index * chunk, chunk)], matrices.at[index], sems.at[index]
-        )
-        for index in range(chunks)
+        pltpu.make_async_copy(source, matrices.at[index], sems.at[index])
+        for index, source in enumerate(sources)
     ]
     for copy in copies:
         copy.start()
@@ -116,13 +120,20 @@
         ],
         axis=0,
     )
-    images = jnp.dot(left, into_ref[...], preferred_element_type=jnp.float32)
+    images = jnp.dot(left, move_ref[...], preferred_element_type=jnp.float32)
+    place = lax.broadcasted_iota(jnp.int32, (count, LANES), 1) // width
     for group in range(down * parts):
-        for step in range(taken):
-            row = half + group * taken + step
-            shifted[pl.ds(row, count, stride=pitch), :] = images[
-                group * count : (group + 1) * count, step * LANES : (step + 1) * LANES
+        for block in range(taken // segs):
+            value = images[
+                group * count : (group + 1) * count, block * LANES : (block + 1) * LANES
             ]
+            for seg in range(segs):
+                spot = value
+                for other in range(1, segs):
+                    moved = pltpu.roll(value, other * width, axis=1)
+                    spot = jnp.where(place == (seg + other) % segs, moved, spot)
+                row = half + group * taken + block * segs + seg
+                shifted[pl.ds(row, count, stride=pitch), :] = spot
     first = lax.broadcasted_iota(jnp.int32, (rows, LANES), 1) // width
     for channel in range(count):
         if channel % chunk == 0:
@@ -152,22 +163,22 @@
             mixed = mixed + pltpu.roll(part, LANES - seg * width, axis=1)
         x = shifted[base + half : base + half + height, :]
         result[channel * height : (channel + 1) * height, :] = x + mixed
-    left = jnp.concatenate(
-        [
-            jnp.concatenate(
-                [
-                    result[pl.ds(group * taken + step, count, stride=height), :].astype(
-                        jnp.bfloat16
-                    )
-                    for step in range(taken)
-                ],
-                axis=1,
-            )
-            for group in range(down * parts)
-        ],
-        axis=0,
+    lines = []
+    for group in range(down * parts):
+        line = []
+        for start in range(group * taken, (group + 1) * taken, segs):
+            value = result[pl.ds(start, count, stride=height), :]
+            for seg in range(1, segs):
+                other = result[pl.ds(start + seg, count, stride=height), :]
+                value = jnp.where(place == seg, pltpu.roll(other, seg * width, axis=1), value)
+            line.append(value.astype(jnp.bfloat16))
+        lines.append(jnp.concatenate(line, axis=1))
+    moved = lax.dot_general(
+        jnp.concatenate(lines, axis=0),
+        move_ref[...],
+        (((1,), (1,)), ((), ())),
+        preferred_element_type=jnp.float32,
     )
-    moved = jnp.dot(left, back_ref[...], preferred_element_type=jnp.float32)
     for r in range(down):
         for part in range(parts):
             group = r * parts + part
@@ -178,62 +189,62 @@
 
 
 def moves_of(across, tile_cols):
-    taken = LANES // tile_cols
-    width = across * tile_cols
-    lane = jnp.arange(across * LANES)
+    lane = np.arange(across * LANES)
     step, col = lane % LANES // tile_cols, lane // LANES * tile_cols + lane % tile_cols
-    cell = jnp.arange(taken * LANES)
-    same = step[:, None] == (cell // LANES)[None, :]
-    into = same & (col[:, None] == (cell % LANES % width)[None, :])
-    back = same & (col[:, None] == (cell % LANES)[None, :])
-    return into.astype(jnp.bfloat16), back.T.astype(jnp.bfloat16)
-
-
-def spread_moved(matrices, moves, received, half, across, tile_cols):
+    key = jnp.asarray((step * across * tile_cols + col).astype(np.int32))
+    cell = lax.broadcasted_iota(jnp.int32, (across * LANES,) * 2, 1)
+    return (key[:, None] == cell).astype(jnp.bfloat16)
+
+
+def spread_moved(matrices, move, received, half, across, tile_cols):
     devices, count, cells = received.shape
     segs = LANES // (across * tile_cols)
     height = devices // across * cells // tile_cols
-    tiles = matrices.shape[1]
+    tiles = matrices[0].shape[1]
     pitch = height + STEP * tiles * segs
-    chunk = per_step(count, CHUNK)
+    chunk = per_step(matrices[0].shape[0], CHUNK)
     whole = pl.BlockSpec(memory_space=pltpu.VMEM)
     return pl.pallas_call(
         lambda *refs: moved_kernel(*refs, half=half, segs=segs),
-        in_specs=[whole] * 3 + [pl.BlockSpec(memory_space=pl.ANY)],
+        in_specs=[whole] * 2 + [pl.BlockSpec(memory_space=pl.ANY)] * len(matrices),
         out_specs=whole,
         out_shape=jax.ShapeDtypeStruct(received.shape, received.dtype),
         scratch_shapes=[
             pltpu.VMEM((count * pitch, LANES), jnp.float32),
             pltpu.VMEM((count * height, LANES), jnp.float32),
-            pltpu.VMEM((count // chunk, chunk) + matrices.shape[1:], matrices.dtype),
+            pltpu.VMEM((count // chunk, chunk) + matrices[0].shape[1:], matrices[0].dtype),
             pltpu.SemaphoreType.DMA((count // chunk,)),
         ],
         name="depthwise_moved",
-    )(received, *moves, matrices)
-
-
-def matrices_of(taps, width):
+    )(received, move, *matrices)
+
+
+def rows_of(taps, width):
     side, _, count = taps.shape
-    half = (side - 1) // 2
     segs = LANES // width
     groups = -(-side // (STEP * segs)) * segs
     v = jnp.transpose(taps[:, ::-1, :], (2, 0, 1))
     v = jnp.pad(v, ((0, 0), (0, STEP * groups - side), (0, width - side)))
     v = v.reshape(count, groups, STEP, width).transpose(0, 2, 1, 3)
-    v = v.reshape(count, STEP, groups // segs, LANES)
+    return v.reshape(count, STEP, groups // segs, LANES)
+
+
+def matrices_of(v, part, parts, half, width):
+    count = v.shape[0] // parts
+    tiles = v.shape[2]
     several = per_step(count, BUILD)
-    shape = (groups // segs, STEP * width, LANES)
+    steps = count // several
+    shape = (tiles, STEP * width, LANES)
+    size = count * tiles * STEP * width * LANES
     return pl.pallas_call(
         lambda *refs: toeplitz_kernel(*refs, half=half, width=width),
-        grid=(count // several,),
-        in_specs=[pl.BlockSpec((several,) + v.shape[1:], lambda i: (i, 0, 0, 0))],
+        grid=(steps,),
+        in_specs=[
+            pl.BlockSpec((several,) + v.shape[1:], lambda i: (i + part * steps, 0, 0, 0))
+        ],
         out_specs=pl.BlockSpec((several,) + shape, lambda i: (i, 0, 0, 0)),
-        out_shape=jax.ShapeDtypeStruct((count,) + shape, taps.dtype),
-        cost_estimate=pl.CostEstimate(
-            flops=count * groups * STEP * width * width * 4,
-            transcendentals=0,
-            bytes_accessed=count * groups * STEP * width * width * 2,
-        ),
+        out_shape=jax.ShapeDtypeStruct((count,) + shape, v.dtype),
+        cost_estimate=pl.CostEstimate(flops=size * 4, transcendentals=0, bytes_accessed=size * 2),
         name="toeplitz",
     )(v)
 
@@ -345,19 +356,24 @@
     line = [piece] + [turn(piece, "cols", shift) for shift in range(1, across)]
     turned = features.reshape(cells, channels).T.reshape(devices, own, cells)
     images = lax.all_to_all(turned, axes, 0, 0, tiled=True)
-    matrices = matrices_of(dw_kernel, across * tile_cols)
-    moves = moves_of(across, tile_cols)
-    images, matrices, moves, line = lax.optimization_barrier((images, matrices, moves, line))
+    width = across * tile_cols
+    taps = rows_of(dw_kernel, width)
+    early = matrices_of(taps, 0, 2, half, width)
+    early, line = lax.optimization_barrier((early, line))
     line = jnp.concatenate(line, axis=0)
     others = [turn(line, "rows", shift, 2) for shift in range(1, down // 2)]
     near = [line] + [turn(line, "pages", shift) for shift in range(1, pages)]
+    late = matrices_of(taps, 1, 2, half, width)
+    matrices = [early, late]
+    move = moves_of(across, tile_cols)
+    images, matrices, move = lax.optimization_barrier((images, matrices, move))
     if own % 16 == 0:
-        spread = spread_moved(matrices, moves, images, half, across, tile_cols)
+        spread = spread_moved(matrices, move, images, half, across, tile_cols)
     else:
         images = images.reshape(down, across, own, tile_rows, tile_cols)
         images = images.transpose(2, 0, 3, 1, 4)
         images = images.reshape(own, down * tile_rows, across * tile_cols)
-        spread = spread_of(matrices, images, half)
+        spread = spread_of(jnp.concatenate(matrices, axis=0), images, half)
         spread = spread.reshape(own, down, tile_rows, across, tile_cols)
         spread = spread.transpose(1, 3, 0, 2, 4).reshape(devices, own, cells)
     last = [turn(other, "pages", shift) for other in others for shift in range(1, pages)]

time: 84.9 us -> 84.6 us (level)
  other arithmetic: 3.97 us -> 1.87 us
  local copies, waits for them, and re-layouts: 5.37 us -> 7.1 us
    convert_element_type x2 -> x1, other arithmetic: 2.98 us -> 0.94 us  [moves_of(): return (key[:, None] == cell).astype(jnp.bfloat16)]
    rev x1, local copies, waits for them, and re-layouts: 0.2 us -> 1.13 us  [rows_of(): v = jnp.transpose(taps[:, ::-1, :], (2, 0, 1))]
    pallas_call x1 -> x2, Pallas kernels: 11.7 us -> 12 us  [matrices_of(): pl.pallas_call(lambda *refs: toeplitz_kernel(*refs, half=half, width=widt...]
  transfers between devices with their start and end apart: 12 -> 12, of which waited for: 2 -> 2; matrix products, arithmetic and copies ran while one was open for 8% -> 7% of each run, Pallas kernels for 29% -> 29%
where the time goes in v3:
time: 84.6 us; the launch traced here: 84 us
  Pallas kernels  28.6 us (34%)
  waiting for transfers between devices  25.7 us (30%)
  starting transfers between devices  20.6 us (24%)
  local copies, waits for them, and re-layouts  7.1 us (8%)
  other arithmetic  1.87 us (2%)
    ppermute x6, waiting for transfers between devices, turn(): lax.ppermute(array, axis, [(i, (i + shift * within) % size) for i in rang...  25.7 us
    pallas_call x2, Pallas kernels, matrices_of(): pl.pallas_call(lambda *refs: toeplitz_kernel(*refs, half=half, width=widt...  12 us
    ppermute x6, starting transfers between devices, turn(): lax.ppermute(array, axis, [(i, (i + shift * within) % size) for i in rang...  10.2 us
    pallas_call x1, Pallas kernels, spread_moved(): pl.pallas_call(lambda *refs: moved_kernel(*refs, half=half, segs=segs), i...  8.21 us
    all_to_all x1, starting transfers between devices, on_tile(): images = lax.all_to_all(turned, axes, 0, 0, tiled=True)  5.12 us
    all_to_all x1, starting transfers between devices, on_tile(): spread = lax.all_to_all(spread, axes, 0, 0, tiled=True)  4.65 us
    pallas_call x1, Pallas kernels, block_of(): pl.pallas_call(first_kernel, in_specs=[whole] * (1 + len(near)), out_spec...  4.3 us
    pallas_call x1, Pallas kernels, block_of(): pl.pallas_call(second_kernel, in_specs=[whole] * (2 + len(far)), out_spec...  4.06 us
  transfers between devices with their start and end apart: 12, of which 2 were waited for; matrix products, arithmetic and copies ran while one was open for 7% of the time, Pallas kernels for 29%

profile of v3, /device:TPU:0, one launch (start us, length us, event | category | flops | bytes accessed | tf_op | source)
XLA Modules:
  0.0 84.0 jit_solution(4295085219457704350)
XLA Ops:
  0.0 0.9 %fusion.2 = bf16[1,2,48,768]{3,2,1,0:T(8,128)(2,1)S(1)} fusion(s32[]{:T(128)S(6)} %select_n.3, bf16[1,96,768]{2,1,0:T(8,128)(2,1)} %bitcast.22, bf16[1,96,768]{2,1,0:T(8,128)(2,1)} %bitcast.23), kind=kLoop, calls=%fused_computation.5 | loop fusion | flops 294912 | bytes 442372 | tf_op jit(solution)/shard_map/dynamic_slice | solution.py:355
  0.9 5.1 %collective-permute-start.2 = (bf16[1,2,48,768]{3,2,1,0:T(8,128)(2,1)S(1)}, bf16[1,2,48,768]{3,2,1,0:T(8,128)(2,1)S(1)}, u32[]{:S(2)}, u32[]{:S(2)}) collective-permute-start(bf16[1,2,48,768]{3,2,1,0:T(8,128)(2,1)S(1)} %fusion.2), channel_id=1, source_target_pairs={{0,3},{1,0},{2,1},{3,2},{4,7},{5,4},{6,5},{7,6},{8,11},{9,8},{10,9... | collective-permute-start | bytes 442376 | tf_op jit(solution)/shard_map/ppermute | solution.py:333
  6.1 1.0 %collective-permute-start = (bf16[1,2,48,768]{3,2,1,0:T(8,128)(2,1)S(1)}, bf16[1,2,48,768]{3,2,1,0:T(8,128)(2,1)S(1)}, u32[]{:S(2)}, u32[]{:S(2)}) collective-permute-start(bf16[1,2,48,768]{3,2,1,0:T(8,128)(2,1)S(1)} %fusion.2), channel_id=1, source_target_pairs={{0,1},{1,2},{2,3},{3,0},{4,5},{5,6},{6,7},{7,4},{8,9},{9,10},{10,1... | collective-permute-start | bytes 442376 | tf_op jit(solution)/shard_map/ppermute | solution.py:333
  7.1 1.9 %copy.6 = bf16[256,768]{0,1:T(8,128)(2,1)} copy(bf16[256,768]{1,0:T(8,128)(2,1)} %bitcast.21) | data formatting | bytes 786432 | tf_op jit(solution)/shard_map/reshape | solution.py:357
  9.0 5.1 %all-to-all-start = ((bf16[16,48,256]{2,1,0:T(8,128)(2,1)}), bf16[16,48,256]{2,1,0:T(8,128)(2,1)S(1)}, u32[]{:S(2)}, u32[]{:S(2)}) async-start(bf16[16,48,256]{2,1,0:T(8,128)(2,1)} %bitcast.2), calls=%async_computation | async-start | bytes 786432 | tf_op jit(solution)/shard_map/all_to_all | solution.py:358
  14.1 1.1 %rev.3 = bf16[31,31,48]{2,1,0:T(8,128)(2,1)S(1)} reverse(bf16[31,31,48]{2,1,0:T(8,128)(2,1)} %param.6), dimensions={1} | reverse | bytes 184512 | tf_op jit(solution)/shard_map/rev | solution.py:226
  15.4 0.6 copy.7
  16.0 0.9 %reshape.23.refs_0_ = bf16[48,8,2,128]{3,2,1,0:T(2,128)(2,1)} reshape(bf16[48,8,4,64]{3,2,1,0:T(4,128)(2,1)S(1)} %bitcast.18) | data formatting | bytes 393216 | tf_op jit(solution)/shard_map/reshape | solution.py:229
  16.9 6.0 %toeplitz.2.refs_2_ = bf16[24,2,512,128]{3,2,1,0:T(8,128)(2,1)} custom-call(bf16[48,8,2,128]{3,2,1,0:T(2,128)(2,1)} %reshape.23.refs_0_), custom_call_target="tpu_custom_call" | custom-call | flops 12582912 | bytes 6291456 | tf_op jit(solution)/shard_map/toeplitz/pallas_call | solution.py:239
  23.0 2.0 %collective-permute-start.3 = (bf16[4,2,48,768]{3,2,1,0:T(8,128)(2,1)S(1)}, bf16[4,2,48,768]{3,2,1,0:T(8,128)(2,1)S(1)}, u32[]{:S(2)}, u32[]{:S(2)}) collective-permute-start(bf16[4,2,48,768]{3,2,1,0:T(8,128)(2,1)S(1)} %constant_dynamic-update-slice_fusion.refs_1_), channel_id=1, source_target_pairs={{0,8},{4,12},{8,0},{12,4},{1,9},{5,13},{9,1},{13,5},{2,10},{6,14},... | collective-permute-start | bytes 1769480 | tf_op jit(solution)/shard_map/ppermute | solution.py:333
  25.0 6.0 %toeplitz.3.refs_3_ = bf16[24,2,512,128]{3,2,1,0:T(8,128)(2,1)} custom-call(bf16[48,8,2,128]{3,2,1,0:T(2,128)(2,1)} %reshape.23.refs_0_), custom_call_target="tpu_custom_call" | custom-call | flops 12582912 | bytes 6291456 | tf_op jit(solution)/shard_map/toeplitz/pallas_call | solution.py:239
  31.0 0.9 %fusion.refs_1_ = bf16[512,512]{1,0:T(8,128)(2,1)} fusion(s32[512]{0:T(512)S(1)} %copy-done.7), kind=kLoop, calls=%fused_computation.1 | loop fusion | flops 524288 | bytes 526336 | tf_op jit(solution)/shard_map/convert_element_type | solution.py:196
  31.9 0.7 copy-done.1
  32.7 8.2 %depthwise_moved.1 = bf16[16,48,256]{2,1,0:T(8,128)(2,1)} custom-call(bf16[16,48,256]{2,1,0:T(8,128)(2,1)} %copy-done.1, bf16[512,512]{1,0:T(8,128)(2,1)} %fusion.refs_1_, bf16[24,2,512,128]{3,2,1,0:T(8,128)(2,1)} %toeplitz.2.refs_2_, bf16[24,2,512,128]{3,2,1,0:T(8,128)(2,1)} %toeplitz.3.refs_3_), custom_call_target="tpu_custom_call" | custom-call | tf_op jit(solution)/shard_map/depthwise_moved/pallas_call | solution.py:207
  40.9 4.7 %all-to-all-start.1 = ((bf16[16,48,256]{2,1,0:T(8,128)(2,1)}), bf16[16,48,256]{2,1,0:T(8,128)(2,1)S(1)}, u32[]{:S(2)}, u32[]{:S(2)}) async-start(bf16[16,48,256]{2,1,0:T(8,128)(2,1)} %depthwise_moved.1), calls=%async_computation.1 | async-start | bytes 786432 | tf_op jit(solution)/shard_map/all_to_all | solution.py:382
  45.5 1.6 %collective-permute-start.5 = (bf16[4,2,48,768]{3,2,1,0:T(8,128)(2,1)S(1)}, bf16[4,2,48,768]{3,2,1,0:T(8,128)(2,1)S(1)}, u32[]{:S(2)}, u32[]{:S(2)}) collective-permute-start(bf16[4,2,48,768]{3,2,1,0:T(8,128)(2,1)S(1)} %constant_dynamic-update-slice_fusion.refs_1_), channel_id=1, source_target_pairs={{0,16},{16,0},{1,17},{17,1},{2,18},{18,2},{3,19},{19,3},{4,20},{20... | collective-permute-start | bytes 1769480 | tf_op jit(solution)/shard_map/ppermute | solution.py:333
  47.1 0.5 collective-permute-start.4
  47.6 0.5 collective-permute-start.8
  48.1 13.7 %collective-permute-done.5.refs_2_ = bf16[4,2,48,768]{3,2,1,0:T(8,128)(2,1)S(1)} collective-permute-done((bf16[4,2,48,768]{3,2,1,0:T(8,128)(2,1)S(1)}, bf16[4,2,48,768]{3,2,1,0:T(8,128)(2,1)S(1)}, u32[]{:S(2)}, u32[]{:S(2)}) %collective-permute-start.5) | collective-permute-done | bytes 589856 | tf_op jit(solution)/shard_map/ppermute | solution.py:333
  61.8 12.0 %collective-permute-done.4.refs_4_ = bf16[4,2,48,768]{3,2,1,0:T(8,128)(2,1)S(1)} collective-permute-done((bf16[4,2,48,768]{3,2,1,0:T(8,128)(2,1)S(1)}, bf16[4,2,48,768]{3,2,1,0:T(8,128)(2,1)S(1)}, u32[]{:S(2)}, u32[]{:S(2)}) %collective-permute-start.4) | collective-permute-done | bytes 589856 | tf_op jit(solution)/shard_map/ppermute | solution.py:333
  73.9 0.7 copy-done.5
  74.8 4.3 %feed_forward_near.1 = (bf16[256,768]{1,0:T(8,128)(2,1)}, f32[256,768]{1,0:T(8,128)}) custom-call(bf16[768,256]{1,0:T(8,128)(2,1)} %bitcast.19, bf16[4,2,48,768]{3,2,1,0:T(8,128)(2,1)} %copy-done.2, bf16[4,2,48,768]{3,2,1,0:T(8,128)(2,1)} %copy-done.6, bf16[4,2,48,768]{3,2,1,0:T(8,128)(2,1)} %copy-done.3, bf16[4,2,48,768]{3,2,1,0:T(8,128)(2,1)} %copy-done.5), custom_call_target="tpu_custom_call" | custom-call | tf_op jit(solution)/shard_map/feed_forward_near/pallas_call | solution.py:312
  79.1 0.8 copy-done.4
  79.9 4.1 %feed_forward_far.1 = bf16[256,768]{1,0:T(8,128)(2,1)} custom-call(bf16[256,768]{1,0:T(8,128)(2,1)} %get-tuple-element.29.refs_0_, f32[256,768]{1,0:T(8,128)} %get-tuple-element.30.refs_1_, bf16[4,2,48,768]{3,2,1,0:T(8,128)(2,1)} %copy-done.4, bf16[4,2,48,768]{3,2,1,0:T(8,128)(2,1)} %collective-permute-done.7.refs_3_, ...), custom_call_target="tpu_custom_call" | custom-call | tf_op jit(solution)/shard_map/feed_forward_far/pallas_call | solution.py:322
  (32 shorter events, 0.4 us)
Async XLA Ops:
  0.9 21.9 %collective-permute-start.2 = (bf16[1,2,48,768]{3,2,1,0:T(8,128)(2,1)S(1)}, bf16[1,2,48,768]{3,2,1,0:T(8,128)(2,1)S(1)}, u32[]{:S(2)}, u32[]{:S(2)}) collective-permute-start(bf16[1,2,48,768]{3,2,1,0:T(8,128)(2,1)S(1)} %fusion.2), channel_id=1, source_target_pairs={{0,3},{1,0},{2,1},{3,2},{4,7},{5,4},{6,5},{7,6},{8,11},{9,8},{10,9... | collective-permute-start | bytes 442376 | tf_op jit(solution)/shard_map/ppermute | solution.py:333
  6.1 16.8 %collective-permute-start.1 = (bf16[1,2,48,768]{3,2,1,0:T(8,128)(2,1)S(1)}, bf16[1,2,48,768]{3,2,1,0:T(8,128)(2,1)S(1)}, u32[]{:S(2)}, u32[]{:S(2)}) collective-permute-start(bf16[1,2,48,768]{3,2,1,0:T(8,128)(2,1)S(1)} %fusion.2), channel_id=1, source_target_pairs={{0,2},{1,3},{2,0},{3,1},{4,6},{5,7},{6,4},{7,5},{8,10},{9,11},{10,... | collective-permute-start | bytes 442376 | tf_op jit(solution)/shard_map/ppermute | solution.py:333
  6.1 16.8 %collective-permute-start = (bf16[1,2,48,768]{3,2,1,0:T(8,128)(2,1)S(1)}, bf16[1,2,48,768]{3,2,1,0:T(8,128)(2,1)S(1)}, u32[]{:S(2)}, u32[]{:S(2)}) collective-permute-start(bf16[1,2,48,768]{3,2,1,0:T(8,128)(2,1)S(1)} %fusion.2), channel_id=1, source_target_pairs={{0,1},{1,2},{2,3},{3,0},{4,5},{5,6},{6,7},{7,4},{8,9},{9,10},{10,1... | collective-permute-start | bytes 442376 | tf_op jit(solution)/shard_map/ppermute | solution.py:333
  9.0 22.9 %all-to-all-start = ((bf16[16,48,256]{2,1,0:T(8,128)(2,1)}), bf16[16,48,256]{2,1,0:T(8,128)(2,1)S(1)}, u32[]{:S(2)}, u32[]{:S(2)}) async-start(bf16[16,48,256]{2,1,0:T(8,128)(2,1)} %bitcast.2), calls=%async_computation | async-start | bytes 786432 | tf_op jit(solution)/shard_map/all_to_all | solution.py:358
  16.9 14.1 %copy-start.7 = (s32[512]{0:T(512)S(1)}, s32[512]{0:T(512)}, u32[]{:S(2)}) copy-start(s32[512]{0:T(512)} %constant.16.clone) | copy-start | bytes 6148
  23.0 24.7 %copy-start.2 = (bf16[4,2,48,768]{3,2,1,0:T(8,128)(2,1)}, bf16[4,2,48,768]{3,2,1,0:T(8,128)(2,1)S(1)}, u32[]{:S(2)}) copy-start(bf16[4,2,48,768]{3,2,1,0:T(8,128)(2,1)S(1)} %constant_dynamic-update-slice_fusion.refs_1_) | copy-start | bytes 1769476
  23.0 24.2 %collective-permute-start.3 = (bf16[4,2,48,768]{3,2,1,0:T(8,128)(2,1)S(1)}, bf16[4,2,48,768]{3,2,1,0:T(8,128)(2,1)S(1)}, u32[]{:S(2)}, u32[]{:S(2)}) collective-permute-start(bf16[4,2,48,768]{3,2,1,0:T(8,128)(2,1)S(1)} %constant_dynamic-update-slice_fusion.refs_1_), channel_id=1, source_target_pairs={{0,8},{4,12},{8,0},{12,4},{1,9},{5,13},{9,1},{13,5},{2,10},{6,14},... | collective-permute-start | bytes 1769480 | tf_op jit(solution)/shard_map/ppermute | solution.py:333
  31.9 0.7 copy-start.1
  40.9 33.0 %all-to-all-start.1 = ((bf16[16,48,256]{2,1,0:T(8,128)(2,1)}), bf16[16,48,256]{2,1,0:T(8,128)(2,1)S(1)}, u32[]{:S(2)}, u32[]{:S(2)}) async-start(bf16[16,48,256]{2,1,0:T(8,128)(2,1)} %depthwise_moved.1), calls=%async_computation.1 | async-start | bytes 786432 | tf_op jit(solution)/shard_map/all_to_all | solution.py:382
  45.5 16.3 %collective-permute-start.5 = (bf16[4,2,48,768]{3,2,1,0:T(8,128)(2,1)S(1)}, bf16[4,2,48,768]{3,2,1,0:T(8,128)(2,1)S(1)}, u32[]{:S(2)}, u32[]{:S(2)}) collective-permute-start(bf16[4,2,48,768]{3,2,1,0:T(8,128)(2,1)S(1)} %constant_dynamic-update-slice_fusion.refs_1_), channel_id=1, source_target_pairs={{0,16},{16,0},{1,17},{17,1},{2,18},{18,2},{3,19},{19,3},{4,20},{20... | collective-permute-start | bytes 1769480 | tf_op jit(solution)/shard_map/ppermute | solution.py:333
  47.1 26.8 %copy-start.3 = (bf16[4,2,48,768]{3,2,1,0:T(8,128)(2,1)}, bf16[4,2,48,768]{3,2,1,0:T(8,128)(2,1)S(1)}, u32[]{:S(2)}) copy-start(bf16[4,2,48,768]{3,2,1,0:T(8,128)(2,1)S(1)} %collective-permute-done.3.refs_3_) | copy-start | bytes 1769476
  47.1 26.7 %collective-permute-start.4 = (bf16[4,2,48,768]{3,2,1,0:T(8,128)(2,1)S(1)}, bf16[4,2,48,768]{3,2,1,0:T(8,128)(2,1)S(1)}, u32[]{:S(2)}, u32[]{:S(2)}) collective-permute-start(bf16[4,2,48,768]{3,2,1,0:T(8,128)(2,1)S(1)} %collective-permute-done.3.refs_3_), channel_id=1, source_target_pairs={{0,16},{16,0},{1,17},{17,1},{2,18},{18,2},{3,19},{19,3},{4,20},{20... | collective-permute-start | bytes 1769480 | tf_op jit(solution)/shard_map/ppermute | solution.py:333
  47.6 31.4 %collective-permute-start.6 = (bf16[4,2,48,768]{3,2,1,0:T(8,128)(2,1)S(1)}, bf16[4,2,48,768]{3,2,1,0:T(8,128)(2,1)S(1)}, u32[]{:S(2)}, u32[]{:S(2)}) collective-permute-start(bf16[4,2,48,768]{3,2,1,0:T(8,128)(2,1)S(1)} %constant_dynamic-update-slice_fusion.refs_1_), channel_id=1, source_target_pairs={{0,4},{4,0},{8,12},{12,8},{1,5},{5,1},{9,13},{13,9},{2,6},{6,2},{1... | collective-permute-start | bytes 1769480 | tf_op jit(solution)/shard_map/ppermute | solution.py:340
  47.6 31.4 %collective-permute-start.8 = (bf16[4,2,48,768]{3,2,1,0:T(8,128)(2,1)S(1)}, bf16[4,2,48,768]{3,2,1,0:T(8,128)(2,1)}, u32[]{:S(2)}, u32[]{:S(2)}) collective-permute-start(bf16[4,2,48,768]{3,2,1,0:T(8,128)(2,1)S(1)} %collective-permute-done.3.refs_3_), channel_id=1, source_target_pairs={{0,4},{4,0},{8,12},{12,8},{1,5},{5,1},{9,13},{13,9},{2,6},{6,2},{1... | collective-permute-start | bytes 1769480 | tf_op jit(solution)/shard_map/ppermute | solution.py:340
  61.8 12.1 %copy-start.6 = (bf16[4,2,48,768]{3,2,1,0:T(8,128)(2,1)}, bf16[4,2,48,768]{3,2,1,0:T(8,128)(2,1)S(1)}, u32[]{:S(2)}) copy-start(bf16[4,2,48,768]{3,2,1,0:T(8,128)(2,1)S(1)} %collective-permute-done.5.refs_2_) | copy-start | bytes 1769476
  61.8 17.3 %collective-permute-start.7 = (bf16[4,2,48,768]{3,2,1,0:T(8,128)(2,1)S(1)}, bf16[4,2,48,768]{3,2,1,0:T(8,128)(2,1)}, u32[]{:S(2)}, u32[]{:S(2)}) collective-permute-start(bf16[4,2,48,768]{3,2,1,0:T(8,128)(2,1)S(1)} %collective-permute-done.5.refs_2_), channel_id=1, source_target_pairs={{0,4},{4,0},{8,12},{12,8},{1,5},{5,1},{9,13},{13,9},{2,6},{6,2},{1... | collective-permute-start | bytes 1769480 | tf_op jit(solution)/shard_map/ppermute | solution.py:340
  73.8 0.8 copy-start.5
  73.8 0.9 %copy-start = (bf16[16,48,256]{2,1,0:T(8,128)(2,1)}, bf16[16,48,256]{2,1,0:T(8,128)(2,1)S(1)}, u32[]{:S(2)}) copy-start(bf16[16,48,256]{2,1,0:T(8,128)(2,1)S(1)} %all-to-all-done.1) | copy-start | bytes 1179652
  73.8 5.3 %collective-permute-start.9 = (bf16[4,2,48,768]{3,2,1,0:T(8,128)(2,1)S(1)}, bf16[4,2,48,768]{3,2,1,0:T(8,128)(2,1)}, u32[]{:S(2)}, u32[]{:S(2)}) collective-permute-start(bf16[4,2,48,768]{3,2,1,0:T(8,128)(2,1)S(1)} %collective-permute-done.4.refs_4_), channel_id=1, source_target_pairs={{0,4},{4,0},{8,12},{12,8},{1,5},{5,1},{9,13},{13,9},{2,6},{6,2},{1... | collective-permute-start | bytes 1769480 | tf_op jit(solution)/shard_map/ppermute | solution.py:340
  79.1 0.8 copy-start.4

commit v4 on v3

--- a/solution.py
+++ b/solution.py
@@ -269,16 +269,16 @@
 
 
 def add_hidden(total, normed, piece_refs):
-    for ref in piece_refs:
-        count, _, units, channels = ref.shape
-        up = ref[:, 0].reshape(count * units, channels)
-        down = ref[:, 1].reshape(count * units, channels)
-        hidden = lax.dot_general(
-            normed, up, (((1,), (1,)), ((), ())), preferred_element_type=jnp.float32
-        )
-        hidden = (0.5 * hidden * (1.0 + lax.erf(hidden * 0.5**0.5))).astype(jnp.bfloat16)
-        total = total + jnp.dot(hidden, down, preferred_element_type=jnp.float32)
-    return total
+    channels = normed.shape[1]
+    up, down = [
+        jnp.concatenate([ref[:, side].reshape(-1, channels) for ref in piece_refs], axis=0)
+        for side in range(2)
+    ]
+    hidden = lax.dot_general(
+        normed, up, (((1,), (1,)), ((), ())), preferred_element_type=jnp.float32
+    )
+    hidden = (0.5 * hidden * (1.0 + lax.erf(hidden * 0.5**0.5))).astype(jnp.bfloat16)
+    return total + jnp.dot(hidden, down, preferred_element_type=jnp.float32)
 
 
 def first_kernel(*refs):
@@ -317,6 +317,7 @@
             jax.ShapeDtypeStruct((cells, channels), spread.dtype),
             jax.ShapeDtypeStruct((cells, channels), jnp.float32),
         ],
+        compiler_params=pltpu.CompilerParams(vmem_limit_bytes=16 << 20),
         name="feed_forward_near",
     )(spread, *near)
     return pl.pallas_call(
@@ -324,6 +325,7 @@
         in_specs=[whole] * (2 + len(far)),
         out_specs=whole,
         out_shape=jax.ShapeDtypeStruct((cells, channels), spread.dtype),
+        compiler_params=pltpu.CompilerParams(vmem_limit_bytes=16 << 20),
         name="feed_forward_far",
     )(normed, total, *far)
 

time: 84.6 us -> 79.4 us (0.939)
  Pallas kernels: 28.6 us -> 24.4 us
  local copies, waits for them, and re-layouts: 7.1 us -> 5.43 us
    pallas_call x1, Pallas kernels: 4.3 us -> 1.27 us  [block_of(): pl.pallas_call(first_kernel, in_specs=[whole] * (1 + len(near)), out_spec...]
    unnamed x19 -> x7, local copies, waits for them, and re-layouts: 2.44 us -> 0.79 us
    pallas_call x1, Pallas kernels: 4.06 us -> 2.95 us  [block_of(): pl.pallas_call(second_kernel, in_specs=[whole] * (2 + len(far)), out_spec...]
  transfers between devices with their start and end apart: 12 -> 12, of which waited for: 2 -> 3; matrix products, arithmetic and copies ran while one was open for 7% -> 7% of each run, Pallas kernels for 29% -> 27%
where the time goes in v4:
time: 79.4 us; the launch traced here: 78.8 us
  waiting for transfers between devices  26.4 us (33%)
  Pallas kernels  24.4 us (31%)
  starting transfers between devices  20.5 us (26%)
  local copies, waits for them, and re-layouts  5.43 us (7%)
  other arithmetic  1.92 us (2%)
    ppermute x6, waiting for transfers between devices, turn(): lax.ppermute(array, axis, [(i, (i + shift * within) % size) for i in rang...  25.7 us
    pallas_call x2, Pallas kernels, matrices_of(): pl.pallas_call(lambda *refs: toeplitz_kernel(*refs, half=half, width=widt...  12 us
    ppermute x6, starting transfers between devices, turn(): lax.ppermute(array, axis, [(i, (i + shift * within) % size) for i in rang...  10.2 us
    pallas_call x1, Pallas kernels, spread_moved(): pl.pallas_call(lambda *refs: moved_kernel(*refs, half=half, segs=segs), i...  8.2 us
    all_to_all x1, starting transfers between devices, on_tile(): images = lax.all_to_all(turned, axes, 0, 0, tiled=True)  5.12 us
    all_to_all x1, starting transfers between devices, on_tile(): spread = lax.all_to_all(spread, axes, 0, 0, tiled=True)  4.65 us
    pallas_call x1, Pallas kernels, block_of(): pl.pallas_call(second_kernel, in_specs=[whole] * (2 + len(far)), out_spec...  2.95 us
    reshape x1, local copies, waits for them, and re-layouts, on_tile(): turned = features.reshape(cells, channels).T.reshape(devices, own, cells)  1.91 us
  transfers between devices with their start and end apart: 12, of which 3 were waited for; matrix products, arithmetic and copies ran while one was open for 7% of the time, Pallas kernels for 27%

profile of v4, /device:TPU:0, one launch (start us, length us, event | category | flops | bytes accessed | tf_op | source)
XLA Modules:
  0.0 78.8 jit_solution(12788104691807889776)
XLA Ops:
  0.0 0.9 %fusion.2 = bf16[1,2,48,768]{3,2,1,0:T(8,128)(2,1)S(1)} fusion(s32[]{:T(128)S(6)} %select_n.3, bf16[1,96,768]{2,1,0:T(8,128)(2,1)} %bitcast.22, bf16[1,96,768]{2,1,0:T(8,128)(2,1)} %bitcast.23), kind=kLoop, calls=%fused_computation.5 | loop fusion | flops 294912 | bytes 442372 | tf_op jit(solution)/shard_map/dynamic_slice | solution.py:357
  0.9 5.1 %collective-permute-start.2 = (bf16[1,2,48,768]{3,2,1,0:T(8,128)(2,1)S(1)}, bf16[1,2,48,768]{3,2,1,0:T(8,128)(2,1)S(1)}, u32[]{:S(2)}, u32[]{:S(2)}) collective-permute-start(bf16[1,2,48,768]{3,2,1,0:T(8,128)(2,1)S(1)} %fusion.2), channel_id=1, source_target_pairs={{0,3},{1,0},{2,1},{3,2},{4,7},{5,4},{6,5},{7,6},{8,11},{9,8},{10,9... | collective-permute-start | bytes 442376 | tf_op jit(solution)/shard_map/ppermute | solution.py:335
  6.1 1.0 %collective-permute-start = (bf16[1,2,48,768]{3,2,1,0:T(8,128)(2,1)S(1)}, bf16[1,2,48,768]{3,2,1,0:T(8,128)(2,1)S(1)}, u32[]{:S(2)}, u32[]{:S(2)}) collective-permute-start(bf16[1,2,48,768]{3,2,1,0:T(8,128)(2,1)S(1)} %fusion.2), channel_id=1, source_target_pairs={{0,1},{1,2},{2,3},{3,0},{4,5},{5,6},{6,7},{7,4},{8,9},{9,10},{10,1... | collective-permute-start | bytes 442376 | tf_op jit(solution)/shard_map/ppermute | solution.py:335
  7.1 1.9 %copy.6 = bf16[256,768]{0,1:T(8,128)(2,1)} copy(bf16[256,768]{1,0:T(8,128)(2,1)} %bitcast.21) | data formatting | bytes 786432 | tf_op jit(solution)/shard_map/reshape | solution.py:359
  9.0 5.1 %all-to-all-start = ((bf16[16,48,256]{2,1,0:T(8,128)(2,1)}), bf16[16,48,256]{2,1,0:T(8,128)(2,1)S(1)}, u32[]{:S(2)}, u32[]{:S(2)}) async-start(bf16[16,48,256]{2,1,0:T(8,128)(2,1)} %bitcast.2), calls=%async_computation | async-start | bytes 786432 | tf_op jit(solution)/shard_map/all_to_all | solution.py:360
  14.1 1.1 %rev.3 = bf16[31,31,48]{2,1,0:T(8,128)(2,1)S(1)} reverse(bf16[31,31,48]{2,1,0:T(8,128)(2,1)} %param.6), dimensions={1} | reverse | bytes 184512 | tf_op jit(solution)/shard_map/rev | solution.py:226
  15.2 0.1 pad.4
  15.4 0.6 copy.7
  16.0 0.9 %reshape.23.refs_0_ = bf16[48,8,2,128]{3,2,1,0:T(2,128)(2,1)} reshape(bf16[48,8,4,64]{3,2,1,0:T(4,128)(2,1)S(1)} %bitcast.19) | data formatting | bytes 393216 | tf_op jit(solution)/shard_map/reshape | solution.py:229
  16.9 6.0 %toeplitz.2.refs_2_ = bf16[24,2,512,128]{3,2,1,0:T(8,128)(2,1)} custom-call(bf16[48,8,2,128]{3,2,1,0:T(2,128)(2,1)} %reshape.23.refs_0_), custom_call_target="tpu_custom_call" | custom-call | flops 12582912 | bytes 6291456 | tf_op jit(solution)/shard_map/toeplitz/pallas_call | solution.py:239
  23.0 2.0 %collective-permute-start.3 = (bf16[4,2,48,768]{3,2,1,0:T(8,128)(2,1)S(1)}, bf16[4,2,48,768]{3,2,1,0:T(8,128)(2,1)S(1)}, u32[]{:S(2)}, u32[]{:S(2)}) collective-permute-start(bf16[4,2,48,768]{3,2,1,0:T(8,128)(2,1)S(1)} %constant_dynamic-update-slice_fusion.refs_1_), channel_id=1, source_target_pairs={{0,8},{4,12},{8,0},{12,4},{1,9},{5,13},{9,1},{13,5},{2,10},{6,14},... | collective-permute-start | bytes 1769480 | tf_op jit(solution)/shard_map/ppermute | solution.py:335
  24.9 6.0 %toeplitz.3.refs_3_ = bf16[24,2,512,128]{3,2,1,0:T(8,128)(2,1)} custom-call(bf16[48,8,2,128]{3,2,1,0:T(2,128)(2,1)} %reshape.23.refs_0_), custom_call_target="tpu_custom_call" | custom-call | flops 12582912 | bytes 6291456 | tf_op jit(solution)/shard_map/toeplitz/pallas_call | solution.py:239
  30.9 1.0 %fusion.refs_1_ = bf16[512,512]{1,0:T(8,128)(2,1)} fusion(s32[512]{0:T(512)S(1)} %copy-done.1), kind=kLoop, calls=%fused_computation.1 | loop fusion | flops 524288 | bytes 526336 | tf_op jit(solution)/shard_map/convert_element_type | solution.py:196
  31.9 0.7 copy-done
  32.7 8.2 %depthwise_moved.1 = bf16[16,48,256]{2,1,0:T(8,128)(2,1)} custom-call(bf16[16,48,256]{2,1,0:T(8,128)(2,1)} %copy-done, bf16[512,512]{1,0:T(8,128)(2,1)} %fusion.refs_1_, bf16[24,2,512,128]{3,2,1,0:T(8,128)(2,1)} %toeplitz.2.refs_2_, bf16[24,2,512,128]{3,2,1,0:T(8,128)(2,1)} %toeplitz.3.refs_3_), custom_call_target="tpu_custom_call" | custom-call | tf_op jit(solution)/shard_map/depthwise_moved/pallas_call | solution.py:207
  40.9 4.7 %all-to-all-start.1 = ((bf16[16,48,256]{2,1,0:T(8,128)(2,1)}), bf16[16,48,256]{2,1,0:T(8,128)(2,1)S(1)}, u32[]{:S(2)}, u32[]{:S(2)}) async-start(bf16[16,48,256]{2,1,0:T(8,128)(2,1)} %depthwise_moved.1), calls=%async_computation.1 | async-start | bytes 786432 | tf_op jit(solution)/shard_map/all_to_all | solution.py:384
  45.6 1.6 %collective-permute-start.5 = (bf16[4,2,48,768]{3,2,1,0:T(8,128)(2,1)S(1)}, bf16[4,2,48,768]{3,2,1,0:T(8,128)(2,1)S(1)}, u32[]{:S(2)}, u32[]{:S(2)}) collective-permute-start(bf16[4,2,48,768]{3,2,1,0:T(8,128)(2,1)S(1)} %constant_dynamic-update-slice_fusion.refs_1_), channel_id=1, source_target_pairs={{0,16},{16,0},{1,17},{17,1},{2,18},{18,2},{3,19},{19,3},{4,20},{20... | collective-permute-start | bytes 1769480 | tf_op jit(solution)/shard_map/ppermute | solution.py:335
  47.1 0.5 collective-permute-start.4
  47.7 0.5 collective-permute-start.8
  48.2 13.7 %collective-permute-done.5.refs_2_ = bf16[4,2,48,768]{3,2,1,0:T(8,128)(2,1)S(1)} collective-permute-done((bf16[4,2,48,768]{3,2,1,0:T(8,128)(2,1)S(1)}, bf16[4,2,48,768]{3,2,1,0:T(8,128)(2,1)S(1)}, u32[]{:S(2)}, u32[]{:S(2)}) %collective-permute-start.5) | collective-permute-done | bytes 589856 | tf_op jit(solution)/shard_map/ppermute | solution.py:335
  61.8 12.0 %collective-permute-done.4.refs_4_ = bf16[4,2,48,768]{3,2,1,0:T(8,128)(2,1)S(1)} collective-permute-done((bf16[4,2,48,768]{3,2,1,0:T(8,128)(2,1)S(1)}, bf16[4,2,48,768]{3,2,1,0:T(8,128)(2,1)S(1)}, u32[]{:S(2)}, u32[]{:S(2)}) %collective-permute-start.4) | collective-permute-done | bytes 589856 | tf_op jit(solution)/shard_map/ppermute | solution.py:335
  73.8 1.3 %feed_forward_near.1 = (bf16[256,768]{1,0:T(8,128)(2,1)S(1)}, f32[256,768]{1,0:T(8,128)S(1)}) custom-call(bf16[768,256]{1,0:T(8,128)(2,1)S(1)} %bitcast.17, bf16[4,2,48,768]{3,2,1,0:T(8,128)(2,1)S(1)} %constant_dynamic-update-slice_fusion.refs_1_, bf16[4,2,48,768]{3,2,1,0:T(8,128)(2,1)S(1)} %collective-permute-done.5.refs_2_, ...), custom_call_target="tpu_custom_call" | custom-call | tf_op jit(solution)/shard_map/feed_forward_near/pallas_call | solution.py:312
  75.2 0.7 collective-permute-done.9.refs_5_
  75.9 2.9 %feed_forward_far.1 = bf16[256,768]{1,0:T(8,128)(2,1)} custom-call(bf16[256,768]{1,0:T(8,128)(2,1)S(1)} %get-tuple-element.29.refs_0_, f32[256,768]{1,0:T(8,128)S(1)} %get-tuple-element.30.refs_1_, bf16[4,2,48,768]{3,2,1,0:T(8,128)(2,1)S(1)} %collective-permute-done.6.refs_2_, bf16[4,2,48,768]{3,2,1,0:T(8,128)(2,1)} %collective-permute-done.7.refs_3_, ...), custom_call_target="tpu_custom_call" | custom-call | tf_op jit(solution)/shard_map/feed_forward_far/pallas_call | solution.py:323
  (20 shorter events, 0.1 us)
Async XLA Ops:
  0.9 21.9 %collective-permute-start.2 = (bf16[1,2,48,768]{3,2,1,0:T(8,128)(2,1)S(1)}, bf16[1,2,48,768]{3,2,1,0:T(8,128)(2,1)S(1)}, u32[]{:S(2)}, u32[]{:S(2)}) collective-permute-start(bf16[1,2,48,768]{3,2,1,0:T(8,128)(2,1)S(1)} %fusion.2), channel_id=1, source_target_pairs={{0,3},{1,0},{2,1},{3,2},{4,7},{5,4},{6,5},{7,6},{8,11},{9,8},{10,9... | collective-permute-start | bytes 442376 | tf_op jit(solution)/shard_map/ppermute | solution.py:335
  6.1 16.8 %collective-permute-start.1 = (bf16[1,2,48,768]{3,2,1,0:T(8,128)(2,1)S(1)}, bf16[1,2,48,768]{3,2,1,0:T(8,128)(2,1)S(1)}, u32[]{:S(2)}, u32[]{:S(2)}) collective-permute-start(bf16[1,2,48,768]{3,2,1,0:T(8,128)(2,1)S(1)} %fusion.2), channel_id=1, source_target_pairs={{0,2},{1,3},{2,0},{3,1},{4,6},{5,7},{6,4},{7,5},{8,10},{9,11},{10,... | collective-permute-start | bytes 442376 | tf_op jit(solution)/shard_map/ppermute | solution.py:335
  6.1 16.8 %collective-permute-start = (bf16[1,2,48,768]{3,2,1,0:T(8,128)(2,1)S(1)}, bf16[1,2,48,768]{3,2,1,0:T(8,128)(2,1)S(1)}, u32[]{:S(2)}, u32[]{:S(2)}) collective-permute-start(bf16[1,2,48,768]{3,2,1,0:T(8,128)(2,1)S(1)} %fusion.2), channel_id=1, source_target_pairs={{0,1},{1,2},{2,3},{3,0},{4,5},{5,6},{6,7},{7,4},{8,9},{9,10},{10,1... | collective-permute-start | bytes 442376 | tf_op jit(solution)/shard_map/ppermute | solution.py:335
  9.0 23.0 %all-to-all-start = ((bf16[16,48,256]{2,1,0:T(8,128)(2,1)}), bf16[16,48,256]{2,1,0:T(8,128)(2,1)S(1)}, u32[]{:S(2)}, u32[]{:S(2)}) async-start(bf16[16,48,256]{2,1,0:T(8,128)(2,1)} %bitcast.2), calls=%async_computation | async-start | bytes 786432 | tf_op jit(solution)/shard_map/all_to_all | solution.py:360
  16.9 14.1 %copy-start.1 = (s32[512]{0:T(512)S(1)}, s32[512]{0:T(512)}, u32[]{:S(2)}) copy-start(s32[512]{0:T(512)} %constant.16.clone) | copy-start | bytes 6148
  23.0 24.2 %collective-permute-start.3 = (bf16[4,2,48,768]{3,2,1,0:T(8,128)(2,1)S(1)}, bf16[4,2,48,768]{3,2,1,0:T(8,128)(2,1)S(1)}, u32[]{:S(2)}, u32[]{:S(2)}) collective-permute-start(bf16[4,2,48,768]{3,2,1,0:T(8,128)(2,1)S(1)} %constant_dynamic-update-slice_fusion.refs_1_), channel_id=1, source_target_pairs={{0,8},{4,12},{8,0},{12,4},{1,9},{5,13},{9,1},{13,5},{2,10},{6,14},... | collective-permute-start | bytes 1769480 | tf_op jit(solution)/shard_map/ppermute | solution.py:335
  31.9 0.7 copy-start
  40.9 32.9 %all-to-all-start.1 = ((bf16[16,48,256]{2,1,0:T(8,128)(2,1)}), bf16[16,48,256]{2,1,0:T(8,128)(2,1)S(1)}, u32[]{:S(2)}, u32[]{:S(2)}) async-start(bf16[16,48,256]{2,1,0:T(8,128)(2,1)} %depthwise_moved.1), calls=%async_computation.1 | async-start | bytes 786432 | tf_op jit(solution)/shard_map/all_to_all | solution.py:384
  45.6 16.3 %collective-permute-start.5 = (bf16[4,2,48,768]{3,2,1,0:T(8,128)(2,1)S(1)}, bf16[4,2,48,768]{3,2,1,0:T(8,128)(2,1)S(1)}, u32[]{:S(2)}, u32[]{:S(2)}) collective-permute-start(bf16[4,2,48,768]{3,2,1,0:T(8,128)(2,1)S(1)} %constant_dynamic-update-slice_fusion.refs_1_), channel_id=1, source_target_pairs={{0,16},{16,0},{1,17},{17,1},{2,18},{18,2},{3,19},{19,3},{4,20},{20... | collective-permute-start | bytes 1769480 | tf_op jit(solution)/shard_map/ppermute | solution.py:335
  47.1 26.7 %collective-permute-start.4 = (bf16[4,2,48,768]{3,2,1,0:T(8,128)(2,1)S(1)}, bf16[4,2,48,768]{3,2,1,0:T(8,128)(2,1)S(1)}, u32[]{:S(2)}, u32[]{:S(2)}) collective-permute-start(bf16[4,2,48,768]{3,2,1,0:T(8,128)(2,1)S(1)} %collective-permute-done.3.refs_3_), channel_id=1, source_target_pairs={{0,16},{16,0},{1,17},{17,1},{2,18},{18,2},{3,19},{19,3},{4,20},{20... | collective-permute-start | bytes 1769480 | tf_op jit(solution)/shard_map/ppermute | solution.py:335
  47.7 27.5 %collective-permute-start.6 = (bf16[4,2,48,768]{3,2,1,0:T(8,128)(2,1)S(1)}, bf16[4,2,48,768]{3,2,1,0:T(8,128)(2,1)S(1)}, u32[]{:S(2)}, u32[]{:S(2)}) collective-permute-start(bf16[4,2,48,768]{3,2,1,0:T(8,128)(2,1)S(1)} %constant_dynamic-update-slice_fusion.refs_1_), channel_id=1, source_target_pairs={{0,4},{4,0},{8,12},{12,8},{1,5},{5,1},{9,13},{13,9},{2,6},{6,2},{1... | collective-permute-start | bytes 1769480 | tf_op jit(solution)/shard_map/ppermute | solution.py:342
  47.7 27.5 %collective-permute-start.8 = (bf16[4,2,48,768]{3,2,1,0:T(8,128)(2,1)S(1)}, bf16[4,2,48,768]{3,2,1,0:T(8,128)(2,1)}, u32[]{:S(2)}, u32[]{:S(2)}) collective-permute-start(bf16[4,2,48,768]{3,2,1,0:T(8,128)(2,1)S(1)} %collective-permute-done.3.refs_3_), channel_id=1, source_target_pairs={{0,4},{4,0},{8,12},{12,8},{1,5},{5,1},{9,13},{13,9},{2,6},{6,2},{1... | collective-permute-start | bytes 1769480 | tf_op jit(solution)/shard_map/ppermute | solution.py:342
  61.8 13.3 %collective-permute-start.7 = (bf16[4,2,48,768]{3,2,1,0:T(8,128)(2,1)S(1)}, bf16[4,2,48,768]{3,2,1,0:T(8,128)(2,1)}, u32[]{:S(2)}, u32[]{:S(2)}) collective-permute-start(bf16[4,2,48,768]{3,2,1,0:T(8,128)(2,1)S(1)} %collective-permute-done.5.refs_2_), channel_id=1, source_target_pairs={{0,4},{4,0},{8,12},{12,8},{1,5},{5,1},{9,13},{13,9},{2,6},{6,2},{1... | collective-permute-start | bytes 1769480 | tf_op jit(solution)/shard_map/ppermute | solution.py:342
  73.8 2.0 %collective-permute-start.9 = (bf16[4,2,48,768]{3,2,1,0:T(8,128)(2,1)S(1)}, bf16[4,2,48,768]{3,2,1,0:T(8,128)(2,1)S(1)}, u32[]{:S(2)}, u32[]{:S(2)}) collective-permute-start(bf16[4,2,48,768]{3,2,1,0:T(8,128)(2,1)S(1)} %collective-permute-done.4.refs_4_), channel_id=1, source_target_pairs={{0,4},{4,0},{8,12},{12,8},{1,5},{5,1},{9,13},{13,9},{2,6},{6,2},{1... | collective-permute-start | bytes 1769480 | tf_op jit(solution)/shard_map/ppermute | solution.py:342

commit v5 on v4

--- a/solution.py
+++ b/solution.py
@@ -9,7 +9,6 @@
 
 LANES = 128
 STEP = 8
-BUILD = 8
 CONV = 16
 CHUNK = 8
 
@@ -18,7 +17,7 @@
     return max(n for n in range(1, most + 1) if count % n == 0)
 
 
-def toeplitz_kernel(v_ref, out_ref, *, half, width):
+def toeplitz_kernel(v_ref, out_hbm, built, sem, *, half, width):
     count, steps, tiles, _ = v_ref.shape
     block = 16
     lane = lax.broadcasted_iota(jnp.int32, (block, LANES), 1) % width
@@ -39,10 +38,12 @@
                     start = index * block
                     piece = turned if start == 0 else pltpu.roll(turned, start, axis=1)
                     low = shift * width + start
-                    out_ref[channel, tile, low : low + block, :] = piece * band
+                    built[channel, tile, low : low + block, :] = piece * band
+        pltpu.make_async_copy(built.at[channel], out_hbm.at[channel], sem).start()
         return carry
 
     lax.fori_loop(0, count, build, 0, unroll=per_step(count, 2))
+    pltpu.make_async_copy(built, out_hbm, sem).wait()
 
 
 def conv_kernel(matrix_ref, img_ref, out_ref, shifted, *, half, segs):
@@ -232,18 +233,15 @@
 def matrices_of(v, part, parts, half, width):
     count = v.shape[0] // parts
     tiles = v.shape[2]
-    several = per_step(count, BUILD)
-    steps = count // several
-    shape = (tiles, STEP * width, LANES)
+    shape = (count, tiles, STEP * width, LANES)
     size = count * tiles * STEP * width * LANES
     return pl.pallas_call(
         lambda *refs: toeplitz_kernel(*refs, half=half, width=width),
-        grid=(steps,),
-        in_specs=[
-            pl.BlockSpec((several,) + v.shape[1:], lambda i: (i + part * steps, 0, 0, 0))
-        ],
-        out_specs=pl.BlockSpec((several,) + shape, lambda i: (i, 0, 0, 0)),
-        out_shape=jax.ShapeDtypeStruct((count,) + shape, v.dtype),
+        grid=(1,),
+        in_specs=[pl.BlockSpec((count,) + v.shape[1:], lambda i: (part, 0, 0, 0))],
+        out_specs=pl.BlockSpec(memory_space=pl.ANY),
+        out_shape=jax.ShapeDtypeStruct(shape, v.dtype),
+        scratch_shapes=[pltpu.VMEM(shape, v.dtype), pltpu.SemaphoreType.DMA(())],
         cost_estimate=pl.CostEstimate(flops=size * 4, transcendentals=0, bytes_accessed=size * 2),
         name="toeplitz",
     )(v)

time: 79.4 us -> 78.6 us (0.990)
  Pallas kernels: 24.4 us -> 23.3 us
    pallas_call x2, Pallas kernels: 12 us -> 10.9 us  [matrices_of(): pl.pallas_call(lambda *refs: toeplitz_kernel(*refs, half=half, width=widt...]
  transfers between devices with their start and end apart: 12 -> 12, of which waited for: 3 -> 3; matrix products, arithmetic and copies ran while one was open for 7% -> 7% of each run, Pallas kernels for 27% -> 26%
where the time goes in v5:
time: 78.6 us; the launch traced here: 78 us
  waiting for transfers between devices  26.4 us (34%)
  Pallas kernels  23.3 us (30%)
  starting transfers between devices  20.9 us (27%)
  local copies, waits for them, and re-layouts  5.43 us (7%)
  other arithmetic  1.92 us (2%)
    ppermute x6, waiting for transfers between devices, turn(): lax.ppermute(array, axis, [(i, (i + shift * within) % size) for i in rang...  25.7 us
    pallas_call x2, Pallas kernels, matrices_of(): pl.pallas_call(lambda *refs: toeplitz_kernel(*refs, half=half, width=widt...  10.9 us
    ppermute x6, starting transfers between devices, turn(): lax.ppermute(array, axis, [(i, (i + shift * within) % size) for i in rang...  10.2 us
    pallas_call x1, Pallas kernels, spread_moved(): pl.pallas_call(lambda *refs: moved_kernel(*refs, half=half, segs=segs), i...  8.19 us
    all_to_all x1, starting transfers between devices, on_tile(): images = lax.all_to_all(turned, axes, 0, 0, tiled=True)  5.12 us
    all_to_all x1, starting transfers between devices, on_tile(): spread = lax.all_to_all(spread, axes, 0, 0, tiled=True)  5 us
    pallas_call x1, Pallas kernels, block_of(): pl.pallas_call(second_kernel, in_specs=[whole] * (2 + len(far)), out_spec...  2.94 us
    reshape x1, local copies, waits for them, and re-layouts, on_tile(): turned = features.reshape(cells, channels).T.reshape(devices, own, cells)  1.91 us
  transfers between devices with their start and end apart: 12, of which 3 were waited for; matrix products, arithmetic and copies ran while one was open for 7% of the time, Pallas kernels for 26%

profile of v5, /device:TPU:0, one launch (start us, length us, event | category | flops | bytes accessed | tf_op | source)
XLA Modules:
  0.0 78.0 jit_solution(12871444098714408063)
XLA Ops:
  0.0 0.9 %fusion.2 = bf16[1,2,48,768]{3,2,1,0:T(8,128)(2,1)S(1)} fusion(s32[]{:T(128)S(6)} %select_n.3, bf16[1,96,768]{2,1,0:T(8,128)(2,1)} %bitcast.22, bf16[1,96,768]{2,1,0:T(8,128)(2,1)} %bitcast.23), kind=kLoop, calls=%fused_computation.5 | loop fusion | flops 294912 | bytes 442372 | tf_op jit(solution)/shard_map/dynamic_slice | solution.py:355
  0.9 5.1 %collective-permute-start.2 = (bf16[1,2,48,768]{3,2,1,0:T(8,128)(2,1)S(1)}, bf16[1,2,48,768]{3,2,1,0:T(8,128)(2,1)S(1)}, u32[]{:S(2)}, u32[]{:S(2)}) collective-permute-start(bf16[1,2,48,768]{3,2,1,0:T(8,128)(2,1)S(1)} %fusion.2), channel_id=1, source_target_pairs={{0,3},{1,0},{2,1},{3,2},{4,7},{5,4},{6,5},{7,6},{8,11},{9,8},{10,9... | collective-permute-start | bytes 442376 | tf_op jit(solution)/shard_map/ppermute | solution.py:333
  6.1 1.0 %collective-permute-start = (bf16[1,2,48,768]{3,2,1,0:T(8,128)(2,1)S(1)}, bf16[1,2,48,768]{3,2,1,0:T(8,128)(2,1)S(1)}, u32[]{:S(2)}, u32[]{:S(2)}) collective-permute-start(bf16[1,2,48,768]{3,2,1,0:T(8,128)(2,1)S(1)} %fusion.2), channel_id=1, source_target_pairs={{0,1},{1,2},{2,3},{3,0},{4,5},{5,6},{6,7},{7,4},{8,9},{9,10},{10,1... | collective-permute-start | bytes 442376 | tf_op jit(solution)/shard_map/ppermute | solution.py:333
  7.1 1.9 %copy.6 = bf16[256,768]{0,1:T(8,128)(2,1)} copy(bf16[256,768]{1,0:T(8,128)(2,1)} %bitcast.21) | data formatting | bytes 786432 | tf_op jit(solution)/shard_map/reshape | solution.py:357
  9.0 5.1 %all-to-all-start = ((bf16[16,48,256]{2,1,0:T(8,128)(2,1)}), bf16[16,48,256]{2,1,0:T(8,128)(2,1)S(1)}, u32[]{:S(2)}, u32[]{:S(2)}) async-start(bf16[16,48,256]{2,1,0:T(8,128)(2,1)} %bitcast.2), calls=%async_computation | async-start | bytes 786432 | tf_op jit(solution)/shard_map/all_to_all | solution.py:358
  14.1 1.1 %rev.3 = bf16[31,31,48]{2,1,0:T(8,128)(2,1)S(1)} reverse(bf16[31,31,48]{2,1,0:T(8,128)(2,1)} %param.6), dimensions={1} | reverse | bytes 184512 | tf_op jit(solution)/shard_map/rev | solution.py:227
  15.2 0.1 pad.4
  15.4 0.6 copy.7
  16.0 0.9 %reshape.23.refs_0_ = bf16[48,8,2,128]{3,2,1,0:T(2,128)(2,1)} reshape(bf16[48,8,4,64]{3,2,1,0:T(4,128)(2,1)S(1)} %bitcast.19) | data formatting | bytes 393216 | tf_op jit(solution)/shard_map/reshape | solution.py:230
  16.9 5.4 %toeplitz.2.refs_2_ = bf16[24,2,512,128]{3,2,1,0:T(8,128)(2,1)} custom-call(bf16[48,8,2,128]{3,2,1,0:T(2,128)(2,1)} %reshape.23.refs_0_), custom_call_target="tpu_custom_call" | custom-call | flops 12582912 | bytes 6291456 | tf_op jit(solution)/shard_map/toeplitz/pallas_call | solution.py:238
  22.4 2.0 %collective-permute-start.3 = (bf16[4,2,48,768]{3,2,1,0:T(8,128)(2,1)S(1)}, bf16[4,2,48,768]{3,2,1,0:T(8,128)(2,1)S(1)}, u32[]{:S(2)}, u32[]{:S(2)}) collective-permute-start(bf16[4,2,48,768]{3,2,1,0:T(8,128)(2,1)S(1)} %constant_dynamic-update-slice_fusion.refs_1_), channel_id=1, source_target_pairs={{0,8},{4,12},{8,0},{12,4},{1,9},{5,13},{9,1},{13,5},{2,10},{6,14},... | collective-permute-start | bytes 1769480 | tf_op jit(solution)/shard_map/ppermute | solution.py:333
  24.4 5.4 %toeplitz.3.refs_3_ = bf16[24,2,512,128]{3,2,1,0:T(8,128)(2,1)} custom-call(bf16[48,8,2,128]{3,2,1,0:T(2,128)(2,1)} %reshape.23.refs_0_), custom_call_target="tpu_custom_call" | custom-call | flops 12582912 | bytes 6291456 | tf_op jit(solution)/shard_map/toeplitz/pallas_call | solution.py:238
  29.8 1.0 %fusion.refs_1_ = bf16[512,512]{1,0:T(8,128)(2,1)} fusion(s32[512]{0:T(512)S(1)} %copy-done.1), kind=kLoop, calls=%fused_computation.1 | loop fusion | flops 524288 | bytes 526336 | tf_op jit(solution)/shard_map/convert_element_type | solution.py:197
  30.8 0.7 copy-done
  31.6 8.2 %depthwise_moved.1 = bf16[16,48,256]{2,1,0:T(8,128)(2,1)} custom-call(bf16[16,48,256]{2,1,0:T(8,128)(2,1)} %copy-done, bf16[512,512]{1,0:T(8,128)(2,1)} %fusion.refs_1_, bf16[24,2,512,128]{3,2,1,0:T(8,128)(2,1)} %toeplitz.2.refs_2_, bf16[24,2,512,128]{3,2,1,0:T(8,128)(2,1)} %toeplitz.3.refs_3_), custom_call_target="tpu_custom_call" | custom-call | tf_op jit(solution)/shard_map/depthwise_moved/pallas_call | solution.py:208
  39.8 5.0 %all-to-all-start.1 = ((bf16[16,48,256]{2,1,0:T(8,128)(2,1)}), bf16[16,48,256]{2,1,0:T(8,128)(2,1)S(1)}, u32[]{:S(2)}, u32[]{:S(2)}) async-start(bf16[16,48,256]{2,1,0:T(8,128)(2,1)} %depthwise_moved.1), calls=%async_computation.1 | async-start | bytes 786432 | tf_op jit(solution)/shard_map/all_to_all | solution.py:382
  44.8 1.6 %collective-permute-start.5 = (bf16[4,2,48,768]{3,2,1,0:T(8,128)(2,1)S(1)}, bf16[4,2,48,768]{3,2,1,0:T(8,128)(2,1)S(1)}, u32[]{:S(2)}, u32[]{:S(2)}) collective-permute-start(bf16[4,2,48,768]{3,2,1,0:T(8,128)(2,1)S(1)} %constant_dynamic-update-slice_fusion.refs_1_), channel_id=1, source_target_pairs={{0,16},{16,0},{1,17},{17,1},{2,18},{18,2},{3,19},{19,3},{4,20},{20... | collective-permute-start | bytes 1769480 | tf_op jit(solution)/shard_map/ppermute | solution.py:333
  46.4 0.5 collective-permute-start.4
  46.9 0.5 collective-permute-start.8
  47.4 13.7 %collective-permute-done.5.refs_2_ = bf16[4,2,48,768]{3,2,1,0:T(8,128)(2,1)S(1)} collective-permute-done((bf16[4,2,48,768]{3,2,1,0:T(8,128)(2,1)S(1)}, bf16[4,2,48,768]{3,2,1,0:T(8,128)(2,1)S(1)}, u32[]{:S(2)}, u32[]{:S(2)}) %collective-permute-start.5) | collective-permute-done | bytes 589856 | tf_op jit(solution)/shard_map/ppermute | solution.py:333
  61.1 12.0 %collective-permute-done.4.refs_4_ = bf16[4,2,48,768]{3,2,1,0:T(8,128)(2,1)S(1)} collective-permute-done((bf16[4,2,48,768]{3,2,1,0:T(8,128)(2,1)S(1)}, bf16[4,2,48,768]{3,2,1,0:T(8,128)(2,1)S(1)}, u32[]{:S(2)}, u32[]{:S(2)}) %collective-permute-start.4) | collective-permute-done | bytes 589856 | tf_op jit(solution)/shard_map/ppermute | solution.py:333
  73.1 1.3 %feed_forward_near.1 = (bf16[256,768]{1,0:T(8,128)(2,1)S(1)}, f32[256,768]{1,0:T(8,128)S(1)}) custom-call(bf16[768,256]{1,0:T(8,128)(2,1)S(1)} %bitcast.17, bf16[4,2,48,768]{3,2,1,0:T(8,128)(2,1)S(1)} %constant_dynamic-update-slice_fusion.refs_1_, bf16[4,2,48,768]{3,2,1,0:T(8,128)(2,1)S(1)} %collective-permute-done.5.refs_2_, ...), custom_call_target="tpu_custom_call" | custom-call | tf_op jit(solution)/shard_map/feed_forward_near/pallas_call | solution.py:310
  74.4 0.7 collective-permute-done.9.refs_5_
  75.1 2.9 %feed_forward_far.1 = bf16[256,768]{1,0:T(8,128)(2,1)} custom-call(bf16[256,768]{1,0:T(8,128)(2,1)S(1)} %get-tuple-element.29.refs_0_, f32[256,768]{1,0:T(8,128)S(1)} %get-tuple-element.30.refs_1_, bf16[4,2,48,768]{3,2,1,0:T(8,128)(2,1)S(1)} %collective-permute-done.6.refs_2_, bf16[4,2,48,768]{3,2,1,0:T(8,128)(2,1)} %collective-permute-done.7.refs_3_, ...), custom_call_target="tpu_custom_call" | custom-call | tf_op jit(solution)/shard_map/feed_forward_far/pallas_call | solution.py:321
  (20 shorter events, 0.1 us)
Async XLA Ops:
  0.9 21.4 %collective-permute-start.2 = (bf16[1,2,48,768]{3,2,1,0:T(8,128)(2,1)S(1)}, bf16[1,2,48,768]{3,2,1,0:T(8,128)(2,1)S(1)}, u32[]{:S(2)}, u32[]{:S(2)}) collective-permute-start(bf16[1,2,48,768]{3,2,1,0:T(8,128)(2,1)S(1)} %fusion.2), channel_id=1, source_target_pairs={{0,3},{1,0},{2,1},{3,2},{4,7},{5,4},{6,5},{7,6},{8,11},{9,8},{10,9... | collective-permute-start | bytes 442376 | tf_op jit(solution)/shard_map/ppermute | solution.py:333
  6.1 16.3 %collective-permute-start.1 = (bf16[1,2,48,768]{3,2,1,0:T(8,128)(2,1)S(1)}, bf16[1,2,48,768]{3,2,1,0:T(8,128)(2,1)S(1)}, u32[]{:S(2)}, u32[]{:S(2)}) collective-permute-start(bf16[1,2,48,768]{3,2,1,0:T(8,128)(2,1)S(1)} %fusion.2), channel_id=1, source_target_pairs={{0,2},{1,3},{2,0},{3,1},{4,6},{5,7},{6,4},{7,5},{8,10},{9,11},{10,... | collective-permute-start | bytes 442376 | tf_op jit(solution)/shard_map/ppermute | solution.py:333
  6.1 16.3 %collective-permute-start = (bf16[1,2,48,768]{3,2,1,0:T(8,128)(2,1)S(1)}, bf16[1,2,48,768]{3,2,1,0:T(8,128)(2,1)S(1)}, u32[]{:S(2)}, u32[]{:S(2)}) collective-permute-start(bf16[1,2,48,768]{3,2,1,0:T(8,128)(2,1)S(1)} %fusion.2), channel_id=1, source_target_pairs={{0,1},{1,2},{2,3},{3,0},{4,5},{5,6},{6,7},{7,4},{8,9},{9,10},{10,1... | collective-permute-start | bytes 442376 | tf_op jit(solution)/shard_map/ppermute | solution.py:333
  9.0 21.8 %all-to-all-start = ((bf16[16,48,256]{2,1,0:T(8,128)(2,1)}), bf16[16,48,256]{2,1,0:T(8,128)(2,1)S(1)}, u32[]{:S(2)}, u32[]{:S(2)}) async-start(bf16[16,48,256]{2,1,0:T(8,128)(2,1)} %bitcast.2), calls=%async_computation | async-start | bytes 786432 | tf_op jit(solution)/shard_map/all_to_all | solution.py:358
  16.9 13.0 %copy-start.1 = (s32[512]{0:T(512)S(1)}, s32[512]{0:T(512)}, u32[]{:S(2)}) copy-start(s32[512]{0:T(512)} %constant.16.clone) | copy-start | bytes 6148
  22.4 24.0 %collective-permute-start.3 = (bf16[4,2,48,768]{3,2,1,0:T(8,128)(2,1)S(1)}, bf16[4,2,48,768]{3,2,1,0:T(8,128)(2,1)S(1)}, u32[]{:S(2)}, u32[]{:S(2)}) collective-permute-start(bf16[4,2,48,768]{3,2,1,0:T(8,128)(2,1)S(1)} %constant_dynamic-update-slice_fusion.refs_1_), channel_id=1, source_target_pairs={{0,8},{4,12},{8,0},{12,4},{1,9},{5,13},{9,1},{13,5},{2,10},{6,14},... | collective-permute-start | bytes 1769480 | tf_op jit(solution)/shard_map/ppermute | solution.py:333
  30.8 0.7 copy-start
  39.8 33.3 %all-to-all-start.1 = ((bf16[16,48,256]{2,1,0:T(8,128)(2,1)}), bf16[16,48,256]{2,1,0:T(8,128)(2,1)S(1)}, u32[]{:S(2)}, u32[]{:S(2)}) async-start(bf16[16,48,256]{2,1,0:T(8,128)(2,1)} %depthwise_moved.1), calls=%async_computation.1 | async-start | bytes 786432 | tf_op jit(solution)/shard_map/all_to_all | solution.py:382
  44.8 16.3 %collective-permute-start.5 = (bf16[4,2,48,768]{3,2,1,0:T(8,128)(2,1)S(1)}, bf16[4,2,48,768]{3,2,1,0:T(8,128)(2,1)S(1)}, u32[]{:S(2)}, u32[]{:S(2)}) collective-permute-start(bf16[4,2,48,768]{3,2,1,0:T(8,128)(2,1)S(1)} %constant_dynamic-update-slice_fusion.refs_1_), channel_id=1, source_target_pairs={{0,16},{16,0},{1,17},{17,1},{2,18},{18,2},{3,19},{19,3},{4,20},{20... | collective-permute-start | bytes 1769480 | tf_op jit(solution)/shard_map/ppermute | solution.py:333
  46.4 26.7 %collective-permute-start.4 = (bf16[4,2,48,768]{3,2,1,0:T(8,128)(2,1)S(1)}, bf16[4,2,48,768]{3,2,1,0:T(8,128)(2,1)S(1)}, u32[]{:S(2)}, u32[]{:S(2)}) collective-permute-start(bf16[4,2,48,768]{3,2,1,0:T(8,128)(2,1)S(1)} %collective-permute-done.3.refs_3_), channel_id=1, source_target_pairs={{0,16},{16,0},{1,17},{17,1},{2,18},{18,2},{3,19},{19,3},{4,20},{20... | collective-permute-start | bytes 1769480 | tf_op jit(solution)/shard_map/ppermute | solution.py:333
  46.9 27.5 %collective-permute-start.6 = (bf16[4,2,48,768]{3,2,1,0:T(8,128)(2,1)S(1)}, bf16[4,2,48,768]{3,2,1,0:T(8,128)(2,1)S(1)}, u32[]{:S(2)}, u32[]{:S(2)}) collective-permute-start(bf16[4,2,48,768]{3,2,1,0:T(8,128)(2,1)S(1)} %constant_dynamic-update-slice_fusion.refs_1_), channel_id=1, source_target_pairs={{0,4},{4,0},{8,12},{12,8},{1,5},{5,1},{9,13},{13,9},{2,6},{6,2},{1... | collective-permute-start | bytes 1769480 | tf_op jit(solution)/shard_map/ppermute | solution.py:340
  46.9 27.5 %collective-permute-start.8 = (bf16[4,2,48,768]{3,2,1,0:T(8,128)(2,1)S(1)}, bf16[4,2,48,768]{3,2,1,0:T(8,128)(2,1)}, u32[]{:S(2)}, u32[]{:S(2)}) collective-permute-start(bf16[4,2,48,768]{3,2,1,0:T(8,128)(2,1)S(1)} %collective-permute-done.3.refs_3_), channel_id=1, source_target_pairs={{0,4},{4,0},{8,12},{12,8},{1,5},{5,1},{9,13},{13,9},{2,6},{6,2},{1... | collective-permute-start | bytes 1769480 | tf_op jit(solution)/shard_map/ppermute | solution.py:340
  61.1 13.3 %collective-permute-start.7 = (bf16[4,2,48,768]{3,2,1,0:T(8,128)(2,1)S(1)}, bf16[4,2,48,768]{3,2,1,0:T(8,128)(2,1)}, u32[]{:S(2)}, u32[]{:S(2)}) collective-permute-start(bf16[4,2,48,768]{3,2,1,0:T(8,128)(2,1)S(1)} %collective-permute-done.5.refs_2_), channel_id=1, source_target_pairs={{0,4},{4,0},{8,12},{12,8},{1,5},{5,1},{9,13},{13,9},{2,6},{6,2},{1... | collective-permute-start | bytes 1769480 | tf_op jit(solution)/shard_map/ppermute | solution.py:340
  73.1 2.0 %collective-permute-start.9 = (bf16[4,2,48,768]{3,2,1,0:T(8,128)(2,1)S(1)}, bf16[4,2,48,768]{3,2,1,0:T(8,128)(2,1)S(1)}, u32[]{:S(2)}, u32[]{:S(2)}) collective-permute-start(bf16[4,2,48,768]{3,2,1,0:T(8,128)(2,1)S(1)} %collective-permute-done.4.refs_4_), channel_id=1, source_target_pairs={{0,4},{4,0},{8,12},{12,8},{1,5},{5,1},{9,13},{13,9},{2,6},{6,2},{1... | collective-permute-start | bytes 1769480 | tf_op jit(solution)/shard_map/ppermute | solution.py:340

commit v6 on v5

--- a/solution.py
+++ b/solution.py
@@ -381,8 +381,9 @@
     far = [partner(each, "rows") for each in near]
     spread = lax.all_to_all(spread, axes, 0, 0, tiled=True)
     spread, last = lax.optimization_barrier((spread, last))
-    far += [partner(each, "rows") for each in last]
-    result = block_of(spread.reshape(channels, cells), near + last, far)
+    near = near + last + far
+    far = [partner(each, "rows") for each in last]
+    result = block_of(spread.reshape(channels, cells), near, far)
     return result.reshape(tile_rows, tile_cols, channels)
 
 

time: 78.6 us -> 78.2 us (level)
    pallas_call x1, Pallas kernels: 1.27 us -> 3.13 us  [block_of(): pl.pallas_call(first_kernel, in_specs=[whole] * (1 + len(near)), out_spec...]
    pallas_call x1, Pallas kernels: 2.94 us -> 1.38 us  [block_of(): pl.pallas_call(second_kernel, in_specs=[whole] * (2 + len(far)), out_spec...]
  transfers between devices with their start and end apart: 12 -> 12, of which waited for: 3 -> 2; matrix products, arithmetic and copies ran while one was open for 7% -> 7% of each run, Pallas kernels for 26% -> 29%
where the time goes in v6:
time: 78.2 us; the launch traced here: 77.6 us
  waiting for transfers between devices  25.7 us (33%)
  Pallas kernels  23.6 us (30%)
  starting transfers between devices  20.9 us (27%)
  local copies, waits for them, and re-layouts  5.43 us (7%)
  other arithmetic  1.92 us (2%)
    ppermute x6, waiting for transfers between devices, turn(): lax.ppermute(array, axis, [(i, (i + shift * within) % size) for i in rang...  25.7 us
    pallas_call x2, Pallas kernels, matrices_of(): pl.pallas_call(lambda *refs: toeplitz_kernel(*refs, half=half, width=widt...  10.9 us
    ppermute x6, starting transfers between devices, turn(): lax.ppermute(array, axis, [(i, (i + shift * within) % size) for i in rang...  10.2 us
    pallas_call x1, Pallas kernels, spread_moved(): pl.pallas_call(lambda *refs: moved_kernel(*refs, half=half, segs=segs), i...  8.19 us
    all_to_all x1, starting transfers between devices, on_tile(): images = lax.all_to_all(turned, axes, 0, 0, tiled=True)  5.12 us
    all_to_all x1, starting transfers between devices, on_tile(): spread = lax.all_to_all(spread, axes, 0, 0, tiled=True)  5 us
    pallas_call x1, Pallas kernels, block_of(): pl.pallas_call(first_kernel, in_specs=[whole] * (1 + len(near)), out_spec...  3.13 us
    reshape x1, local copies, waits for them, and re-layouts, on_tile(): turned = features.reshape(cells, channels).T.reshape(devices, own, cells)  1.91 us
  transfers between devices with their start and end apart: 12, of which 2 were waited for; matrix products, arithmetic and copies ran while one was open for 7% of the time, Pallas kernels for 29%

profile of v6, /device:TPU:0, one launch (start us, length us, event | category | flops | bytes accessed | tf_op | source)
XLA Modules:
  0.0 77.6 jit_solution(7511095658559172662)
XLA Ops:
  0.0 0.9 %fusion.2 = bf16[1,2,48,768]{3,2,1,0:T(8,128)(2,1)S(1)} fusion(s32[]{:T(128)S(6)} %select_n.3, bf16[1,96,768]{2,1,0:T(8,128)(2,1)} %bitcast.22, bf16[1,96,768]{2,1,0:T(8,128)(2,1)} %bitcast.23), kind=kLoop, calls=%fused_computation.5 | loop fusion | flops 294912 | bytes 442372 | tf_op jit(solution)/shard_map/dynamic_slice | solution.py:355
  0.9 5.1 %collective-permute-start.2 = (bf16[1,2,48,768]{3,2,1,0:T(8,128)(2,1)S(1)}, bf16[1,2,48,768]{3,2,1,0:T(8,128)(2,1)S(1)}, u32[]{:S(2)}, u32[]{:S(2)}) collective-permute-start(bf16[1,2,48,768]{3,2,1,0:T(8,128)(2,1)S(1)} %fusion.2), channel_id=1, source_target_pairs={{0,3},{1,0},{2,1},{3,2},{4,7},{5,4},{6,5},{7,6},{8,11},{9,8},{10,9... | collective-permute-start | bytes 442376 | tf_op jit(solution)/shard_map/ppermute | solution.py:333
  6.1 1.0 %collective-permute-start = (bf16[1,2,48,768]{3,2,1,0:T(8,128)(2,1)S(1)}, bf16[1,2,48,768]{3,2,1,0:T(8,128)(2,1)S(1)}, u32[]{:S(2)}, u32[]{:S(2)}) collective-permute-start(bf16[1,2,48,768]{3,2,1,0:T(8,128)(2,1)S(1)} %fusion.2), channel_id=1, source_target_pairs={{0,1},{1,2},{2,3},{3,0},{4,5},{5,6},{6,7},{7,4},{8,9},{9,10},{10,1... | collective-permute-start | bytes 442376 | tf_op jit(solution)/shard_map/ppermute | solution.py:333
  7.1 1.9 %copy.6 = bf16[256,768]{0,1:T(8,128)(2,1)} copy(bf16[256,768]{1,0:T(8,128)(2,1)} %bitcast.21) | data formatting | bytes 786432 | tf_op jit(solution)/shard_map/reshape | solution.py:357
  9.0 5.1 %all-to-all-start = ((bf16[16,48,256]{2,1,0:T(8,128)(2,1)}), bf16[16,48,256]{2,1,0:T(8,128)(2,1)S(1)}, u32[]{:S(2)}, u32[]{:S(2)}) async-start(bf16[16,48,256]{2,1,0:T(8,128)(2,1)} %bitcast.2), calls=%async_computation | async-start | bytes 786432 | tf_op jit(solution)/shard_map/all_to_all | solution.py:358
  14.1 1.1 %rev.3 = bf16[31,31,48]{2,1,0:T(8,128)(2,1)S(1)} reverse(bf16[31,31,48]{2,1,0:T(8,128)(2,1)} %param.6), dimensions={1} | reverse | bytes 184512 | tf_op jit(solution)/shard_map/rev | solution.py:227
  15.2 0.1 pad.4
  15.4 0.6 copy.7
  16.0 0.9 %reshape.23.refs_0_ = bf16[48,8,2,128]{3,2,1,0:T(2,128)(2,1)} reshape(bf16[48,8,4,64]{3,2,1,0:T(4,128)(2,1)S(1)} %bitcast.19) | data formatting | bytes 393216 | tf_op jit(solution)/shard_map/reshape | solution.py:230
  16.9 5.4 %toeplitz.2.refs_2_ = bf16[24,2,512,128]{3,2,1,0:T(8,128)(2,1)} custom-call(bf16[48,8,2,128]{3,2,1,0:T(2,128)(2,1)} %reshape.23.refs_0_), custom_call_target="tpu_custom_call" | custom-call | flops 12582912 | bytes 6291456 | tf_op jit(solution)/shard_map/toeplitz/pallas_call | solution.py:238
  22.3 0.0 collective-permute-done.2
  22.4 2.0 %collective-permute-start.3 = (bf16[4,2,48,768]{3,2,1,0:T(8,128)(2,1)S(1)}, bf16[4,2,48,768]{3,2,1,0:T(8,128)(2,1)S(1)}, u32[]{:S(2)}, u32[]{:S(2)}) collective-permute-start(bf16[4,2,48,768]{3,2,1,0:T(8,128)(2,1)S(1)} %constant_dynamic-update-slice_fusion.refs_1_), channel_id=1, source_target_pairs={{0,8},{4,12},{8,0},{12,4},{1,9},{5,13},{9,1},{13,5},{2,10},{6,14},... | collective-permute-start | bytes 1769480 | tf_op jit(solution)/shard_map/ppermute | solution.py:333
  24.4 5.4 %toeplitz.3.refs_3_ = bf16[24,2,512,128]{3,2,1,0:T(8,128)(2,1)} custom-call(bf16[48,8,2,128]{3,2,1,0:T(2,128)(2,1)} %reshape.23.refs_0_), custom_call_target="tpu_custom_call" | custom-call | flops 12582912 | bytes 6291456 | tf_op jit(solution)/shard_map/toeplitz/pallas_call | solution.py:238
  29.8 1.0 %fusion.refs_1_ = bf16[512,512]{1,0:T(8,128)(2,1)} fusion(s32[512]{0:T(512)S(1)} %copy-done.1), kind=kLoop, calls=%fused_computation.1 | loop fusion | flops 524288 | bytes 526336 | tf_op jit(solution)/shard_map/convert_element_type | solution.py:197
  30.8 0.7 copy-done
  31.6 8.2 %depthwise_moved.1 = bf16[16,48,256]{2,1,0:T(8,128)(2,1)} custom-call(bf16[16,48,256]{2,1,0:T(8,128)(2,1)} %copy-done, bf16[512,512]{1,0:T(8,128)(2,1)} %fusion.refs_1_, bf16[24,2,512,128]{3,2,1,0:T(8,128)(2,1)} %toeplitz.2.refs_2_, bf16[24,2,512,128]{3,2,1,0:T(8,128)(2,1)} %toeplitz.3.refs_3_), custom_call_target="tpu_custom_call" | custom-call | tf_op jit(solution)/shard_map/depthwise_moved/pallas_call | solution.py:208
  39.8 5.0 %all-to-all-start.1 = ((bf16[16,48,256]{2,1,0:T(8,128)(2,1)}), bf16[16,48,256]{2,1,0:T(8,128)(2,1)S(1)}, u32[]{:S(2)}, u32[]{:S(2)}) async-start(bf16[16,48,256]{2,1,0:T(8,128)(2,1)} %depthwise_moved.1), calls=%async_computation.1 | async-start | bytes 786432 | tf_op jit(solution)/shard_map/all_to_all | solution.py:382
  44.8 1.6 %collective-permute-start.5 = (bf16[4,2,48,768]{3,2,1,0:T(8,128)(2,1)S(1)}, bf16[4,2,48,768]{3,2,1,0:T(8,128)(2,1)S(1)}, u32[]{:S(2)}, u32[]{:S(2)}) collective-permute-start(bf16[4,2,48,768]{3,2,1,0:T(8,128)(2,1)S(1)} %constant_dynamic-update-slice_fusion.refs_1_), channel_id=1, source_target_pairs={{0,16},{16,0},{1,17},{17,1},{2,18},{18,2},{3,19},{19,3},{4,20},{20... | collective-permute-start | bytes 1769480 | tf_op jit(solution)/shard_map/ppermute | solution.py:333
  46.4 0.5 collective-permute-start.4
  46.9 0.5 collective-permute-start.8
  47.4 13.7 %collective-permute-done.5.refs_2_ = bf16[4,2,48,768]{3,2,1,0:T(8,128)(2,1)S(1)} collective-permute-done((bf16[4,2,48,768]{3,2,1,0:T(8,128)(2,1)S(1)}, bf16[4,2,48,768]{3,2,1,0:T(8,128)(2,1)S(1)}, u32[]{:S(2)}, u32[]{:S(2)}) %collective-permute-start.5) | collective-permute-done | bytes 589856 | tf_op jit(solution)/shard_map/ppermute | solution.py:333
  61.1 12.0 %collective-permute-done.4.refs_4_ = bf16[4,2,48,768]{3,2,1,0:T(8,128)(2,1)S(1)} collective-permute-done((bf16[4,2,48,768]{3,2,1,0:T(8,128)(2,1)S(1)}, bf16[4,2,48,768]{3,2,1,0:T(8,128)(2,1)S(1)}, u32[]{:S(2)}, u32[]{:S(2)}) %collective-permute-start.4) | collective-permute-done | bytes 589856 | tf_op jit(solution)/shard_map/ppermute | solution.py:333
  73.1 3.1 %feed_forward_near.1 = (bf16[256,768]{1,0:T(8,128)(2,1)S(1)}, f32[256,768]{1,0:T(8,128)S(1)}) custom-call(bf16[768,256]{1,0:T(8,128)(2,1)S(1)} %bitcast.17, bf16[4,2,48,768]{3,2,1,0:T(8,128)(2,1)S(1)} %constant_dynamic-update-slice_fusion.refs_1_, bf16[4,2,48,768]{3,2,1,0:T(8,128)(2,1)S(1)} %collective-permute-done.5.refs_2_, ...), custom_call_target="tpu_custom_call" | custom-call | tf_op jit(solution)/shard_map/feed_forward_near/pallas_call | solution.py:310
  76.3 1.4 %feed_forward_far.1 = bf16[256,768]{1,0:T(8,128)(2,1)} custom-call(bf16[256,768]{1,0:T(8,128)(2,1)S(1)} %get-tuple-element.29.refs_0_, f32[256,768]{1,0:T(8,128)S(1)} %get-tuple-element.30.refs_1_, bf16[4,2,48,768]{3,2,1,0:T(8,128)(2,1)S(1)} %collective-permute-done.9.refs_2_), custom_call_target="tpu_custom_call" | custom-call | tf_op jit(solution)/shard_map/feed_forward_far/pallas_call | solution.py:321
  (20 shorter events, 0.1 us)
Async XLA Ops:
  0.9 21.4 %collective-permute-start.2 = (bf16[1,2,48,768]{3,2,1,0:T(8,128)(2,1)S(1)}, bf16[1,2,48,768]{3,2,1,0:T(8,128)(2,1)S(1)}, u32[]{:S(2)}, u32[]{:S(2)}) collective-permute-start(bf16[1,2,48,768]{3,2,1,0:T(8,128)(2,1)S(1)} %fusion.2), channel_id=1, source_target_pairs={{0,3},{1,0},{2,1},{3,2},{4,7},{5,4},{6,5},{7,6},{8,11},{9,8},{10,9... | collective-permute-start | bytes 442376 | tf_op jit(solution)/shard_map/ppermute | solution.py:333
  6.1 16.3 %collective-permute-start.1 = (bf16[1,2,48,768]{3,2,1,0:T(8,128)(2,1)S(1)}, bf16[1,2,48,768]{3,2,1,0:T(8,128)(2,1)S(1)}, u32[]{:S(2)}, u32[]{:S(2)}) collective-permute-start(bf16[1,2,48,768]{3,2,1,0:T(8,128)(2,1)S(1)} %fusion.2), channel_id=1, source_target_pairs={{0,2},{1,3},{2,0},{3,1},{4,6},{5,7},{6,4},{7,5},{8,10},{9,11},{10,... | collective-permute-start | bytes 442376 | tf_op jit(solution)/shard_map/ppermute | solution.py:333
  6.1 16.3 %collective-permute-start = (bf16[1,2,48,768]{3,2,1,0:T(8,128)(2,1)S(1)}, bf16[1,2,48,768]{3,2,1,0:T(8,128)(2,1)S(1)}, u32[]{:S(2)}, u32[]{:S(2)}) collective-permute-start(bf16[1,2,48,768]{3,2,1,0:T(8,128)(2,1)S(1)} %fusion.2), channel_id=1, source_target_pairs={{0,1},{1,2},{2,3},{3,0},{4,5},{5,6},{6,7},{7,4},{8,9},{9,10},{10,1... | collective-permute-start | bytes 442376 | tf_op jit(solution)/shard_map/ppermute | solution.py:333
  9.0 21.8 %all-to-all-start = ((bf16[16,48,256]{2,1,0:T(8,128)(2,1)}), bf16[16,48,256]{2,1,0:T(8,128)(2,1)S(1)}, u32[]{:S(2)}, u32[]{:S(2)}) async-start(bf16[16,48,256]{2,1,0:T(8,128)(2,1)} %bitcast.2), calls=%async_computation | async-start | bytes 786432 | tf_op jit(solution)/shard_map/all_to_all | solution.py:358
  16.9 13.0 %copy-start.1 = (s32[512]{0:T(512)S(1)}, s32[512]{0:T(512)}, u32[]{:S(2)}) copy-start(s32[512]{0:T(512)} %constant.16.clone) | copy-start | bytes 6148
  22.4 24.0 %collective-permute-start.3 = (bf16[4,2,48,768]{3,2,1,0:T(8,128)(2,1)S(1)}, bf16[4,2,48,768]{3,2,1,0:T(8,128)(2,1)S(1)}, u32[]{:S(2)}, u32[]{:S(2)}) collective-permute-start(bf16[4,2,48,768]{3,2,1,0:T(8,128)(2,1)S(1)} %constant_dynamic-update-slice_fusion.refs_1_), channel_id=1, source_target_pairs={{0,8},{4,12},{8,0},{12,4},{1,9},{5,13},{9,1},{13,5},{2,10},{6,14},... | collective-permute-start | bytes 1769480 | tf_op jit(solution)/shard_map/ppermute | solution.py:333
  30.8 0.7 copy-start
  39.8 33.3 %all-to-all-start.1 = ((bf16[16,48,256]{2,1,0:T(8,128)(2,1)}), bf16[16,48,256]{2,1,0:T(8,128)(2,1)S(1)}, u32[]{:S(2)}, u32[]{:S(2)}) async-start(bf16[16,48,256]{2,1,0:T(8,128)(2,1)} %depthwise_moved.1), calls=%async_computation.1 | async-start | bytes 786432 | tf_op jit(solution)/shard_map/all_to_all | solution.py:382
  44.8 16.3 %collective-permute-start.5 = (bf16[4,2,48,768]{3,2,1,0:T(8,128)(2,1)S(1)}, bf16[4,2,48,768]{3,2,1,0:T(8,128)(2,1)S(1)}, u32[]{:S(2)}, u32[]{:S(2)}) collective-permute-start(bf16[4,2,48,768]{3,2,1,0:T(8,128)(2,1)S(1)} %constant_dynamic-update-slice_fusion.refs_1_), channel_id=1, source_target_pairs={{0,16},{16,0},{1,17},{17,1},{2,18},{18,2},{3,19},{19,3},{4,20},{20... | collective-permute-start | bytes 1769480 | tf_op jit(solution)/shard_map/ppermute | solution.py:333
  46.4 26.7 %collective-permute-start.4 = (bf16[4,2,48,768]{3,2,1,0:T(8,128)(2,1)S(1)}, bf16[4,2,48,768]{3,2,1,0:T(8,128)(2,1)S(1)}, u32[]{:S(2)}, u32[]{:S(2)}) collective-permute-start(bf16[4,2,48,768]{3,2,1,0:T(8,128)(2,1)S(1)} %collective-permute-done.3.refs_3_), channel_id=1, source_target_pairs={{0,16},{16,0},{1,17},{17,1},{2,18},{18,2},{3,19},{19,3},{4,20},{20... | collective-permute-start | bytes 1769480 | tf_op jit(solution)/shard_map/ppermute | solution.py:333
  46.9 26.2 %collective-permute-start.6 = (bf16[4,2,48,768]{3,2,1,0:T(8,128)(2,1)S(1)}, bf16[4,2,48,768]{3,2,1,0:T(8,128)(2,1)S(1)}, u32[]{:S(2)}, u32[]{:S(2)}) collective-permute-start(bf16[4,2,48,768]{3,2,1,0:T(8,128)(2,1)S(1)} %constant_dynamic-update-slice_fusion.refs_1_), channel_id=1, source_target_pairs={{0,4},{4,0},{8,12},{12,8},{1,5},{5,1},{9,13},{13,9},{2,6},{6,2},{1... | collective-permute-start | bytes 1769480 | tf_op jit(solution)/shard_map/ppermute | solution.py:340
  46.9 26.2 %collective-permute-start.8 = (bf16[4,2,48,768]{3,2,1,0:T(8,128)(2,1)S(1)}, bf16[4,2,48,768]{3,2,1,0:T(8,128)(2,1)}, u32[]{:S(2)}, u32[]{:S(2)}) collective-permute-start(bf16[4,2,48,768]{3,2,1,0:T(8,128)(2,1)S(1)} %collective-permute-done.3.refs_3_), channel_id=1, source_target_pairs={{0,4},{4,0},{8,12},{12,8},{1,5},{5,1},{9,13},{13,9},{2,6},{6,2},{1... | collective-permute-start | bytes 1769480 | tf_op jit(solution)/shard_map/ppermute | solution.py:340
  61.1 12.0 %collective-permute-start.7 = (bf16[4,2,48,768]{3,2,1,0:T(8,128)(2,1)S(1)}, bf16[4,2,48,768]{3,2,1,0:T(8,128)(2,1)}, u32[]{:S(2)}, u32[]{:S(2)}) collective-permute-start(bf16[4,2,48,768]{3,2,1,0:T(8,128)(2,1)S(1)} %collective-permute-done.5.refs_2_), channel_id=1, source_target_pairs={{0,4},{4,0},{8,12},{12,8},{1,5},{5,1},{9,13},{13,9},{2,6},{6,2},{1... | collective-permute-start | bytes 1769480 | tf_op jit(solution)/shard_map/ppermute | solution.py:340
  73.1 3.2 %collective-permute-start.9 = (bf16[4,2,48,768]{3,2,1,0:T(8,128)(2,1)S(1)}, bf16[4,2,48,768]{3,2,1,0:T(8,128)(2,1)S(1)}, u32[]{:S(2)}, u32[]{:S(2)}) collective-permute-start(bf16[4,2,48,768]{3,2,1,0:T(8,128)(2,1)S(1)} %collective-permute-done.4.refs_4_), channel_id=1, source_target_pairs={{0,4},{4,0},{8,12},{12,8},{1,5},{5,1},{9,13},{13,9},{2,6},{6,2},{1... | collective-permute-start | bytes 1769480 | tf_op jit(solution)/shard_map/ppermute | solution.py:340
